TPU v7x, 32 devices: a whole 2x2x4 slice. The times are simulated.
32 devices in a mesh: dp: 2 (over x), expert: 16 (over z, y, core).
Axes of the slice: x: 2, y: 2, z: 4, core: 2. Of those that a mesh axis runs over, the one named last changes fastest.
Arguments:
- tokens: bfloat16 [512, 2048], P('expert', 'dp'), may hold values from -6 to 6
- cotangent: bfloat16 [512, 2048], P('expert', 'dp'), may hold values from -6 to 6
- routes: int32 [512, 8], P('expert'), may hold values from 0 to 15, all different within a row; in each aligned block of 32 rows (0 to 31, 32 to 63, ...) at most 20 rows name the same one
- probs: float32 [512, 8], P('expert'), may hold values from 0.03 to 0.6
- matching: int32 [16], replicated, may hold values from 0 to 15, as said below
- gate_weight: bfloat16 [16, 2048, 1024], P('expert', None, 'dp'), may hold values from -0.125 to 0.125
- up_weight: bfloat16 [16, 2048, 1024], P('expert', None, 'dp'), may hold values from -0.125 to 0.125
- down_weight: bfloat16 [16, 2048, 1024], P('expert', None, 'dp'), may hold values from -0.1875 to 0.1875
Outputs:
- input_grad: bfloat16 [512, 2048], P('expert', 'dp')
- gate_weight_grad: float32 [16, 2048, 1024], P('expert', None, 'dp')
- up_weight_grad: float32 [16, 2048, 1024], P('expert', None, 'dp')
- down_weight_grad: float32 [16, 2048, 1024], P('expert', None, 'dp')
Inputs may be any that keep to these rules, and one draw needn't show every extreme that they name: matching pairs the experts: matching[matching[i]] == i and matching[i] != i. `routes`: each token names 8 different experts; within each aligned block of 32 tokens no expert is named by more than 20 tokens.
All inputs are finite; a program needn't handle non-finite values.
Results may differ from a plain program's by a relative error of at most 0.015.
Values may be sent and summed in bfloat16 or wider, within the bound.
A program may use at most 64 MiB of HBM per device.

v0:
```python
import functools

import jax
import jax.numpy as jnp
from jax import lax
from jax.experimental import pallas as pl
from jax.experimental.pallas import tpu as pltpu
from jax.sharding import PartitionSpec as P

contract_rows = (((0,), (0,)), ((), ()))
contract_cols = (((1,), (1,)), ((), ()))
MESH = pl.DeviceIdType.MESH


def bit_count(size):
    return size.bit_length() - 1


def flipped(index, bit):
    step = 2**bit
    return index + step * (1 - 2 * ((index // step) % 2))


def gather_orders(expert_bits, dp_bits):
    far = [("expert", b) for b in range(expert_bits - 1, 1, -1)]
    mid = [("expert", 1)]
    last = [("expert", 0)]
    across = [("dp", b) for b in range(dp_bits)]
    return (
        far + across + mid + last,
        far + mid + across + last,
        across + far + mid + last,
        mid + far + across + last,
        far + mid + last,
    )


def gather_kernel(
    n_expert, n_dp, tokens, cotangent, table, all_tokens, all_cotangent, all_table, send, recv, own
):
    e = lax.axis_index("expert")
    d = lax.axis_index("dp")
    expert_bits, dp_bits = bit_count(n_expert), bit_count(n_dp)
    width = tokens.shape[1]
    half = tokens.shape[0] // 2

    def peer(axis, bit):
        if axis == "expert":
            return (d, flipped(e, bit))
        return (flipped(d, bit), e)

    def held(ref, done, rows, data):
        where = []
        for b in range(expert_bits - 1, -1, -1):
            where.append(slice(None) if ("expert", b) in done else (e // 2**b) % 2)
        where.append(rows)
        if data:
            k = len([x for x in done if x[0] == "dp"])
            start = pl.multiple_of((d // 2**k) * (2**k * width), width)
            where.append(pl.ds(start, 2**k * width))
        else:
            where.append(slice(None))
        return ref.at[tuple(where)]

    barrier = pltpu.get_barrier_semaphore()
    links = [("expert", b) for b in range(expert_bits)] + [("dp", b) for b in range(dp_bits)]
    for link in links:
        pl.semaphore_signal(barrier, inc=1, device_id=peer(*link), device_id_type=MESH)

    orders = gather_orders(expert_bits, dp_bits)
    top, low, whole = pl.ds(0, half), pl.ds(half, half), pl.ds(0, 2 * half)
    parts = [
        (tokens, all_tokens, top, orders[0], True),
        (tokens, all_tokens, low, orders[2], True),
        (cotangent, all_cotangent, top, orders[1], True),
        (cotangent, all_cotangent, low, orders[3], True),
        (table, all_table, whole, orders[4], False),
    ]
    locals_ = []
    for i, (src, dst, rows, order, data) in enumerate(parts):
        c = pltpu.make_async_copy(src.at[rows], held(dst, [], rows, data), own.at[i])
        c.start()
        locals_.append(c)
    pl.semaphore_wait(barrier, len(links))
    flights = [[] for _ in parts]
    steps = max(len(p[3]) for p in parts)
    for s in range(steps):
        turn = (4, 1, 3, 0, 2) if s < 2 else (4, 0, 2, 1, 3)
        for i in turn:
            src, dst, rows, order, data = parts[i]
            if s >= len(order):
                continue
            if s == 0:
                locals_[i].wait()
            else:
                flights[i][s - 1].wait_recv()
            block = held(dst, order[:s], rows, data)
            c = pltpu.make_async_remote_copy(
                src_ref=block,
                dst_ref=block,
                send_sem=send.at[i, s],
                recv_sem=recv.at[i, s],
                device_id=peer(*order[s]),
                device_id_type=MESH,
            )
            c.start()
            flights[i].append(c)
    for f in flights:
        f[-1].wait_recv()
        for c in f:
            c.wait_send()


def gather_all(n_expert, n_dp, tokens, cotangent, table):
    lead = (2,) * bit_count(n_expert)
    rows, width = tokens.shape
    steps = bit_count(n_expert) + bit_count(n_dp)
    wide = jax.ShapeDtypeStruct(lead + (rows, width * n_dp), tokens.dtype)
    small = jax.ShapeDtypeStruct(lead + table.shape, table.dtype)
    outs = pl.pallas_call(
        functools.partial(gather_kernel, n_expert, n_dp),
        out_shape=(wide, wide, small),
        in_specs=[pl.BlockSpec(memory_space=pltpu.VMEM)] * 3,
        out_specs=[pl.BlockSpec(memory_space=pltpu.VMEM)] * 3,
        scratch_shapes=[
            pltpu.SemaphoreType.DMA((5, steps)),
            pltpu.SemaphoreType.DMA((5, steps)),
            pltpu.SemaphoreType.DMA((5,)),
        ],
        compiler_params=pltpu.CompilerParams(collective_id=0, has_side_effects=True),
    )(tokens, cotangent, table)
    total = n_expert * rows
    return (
        outs[0].reshape(total, width * n_dp),
        outs[1].reshape(total, width * n_dp),
        outs[2].reshape(total, table.shape[1]),
    )


def reduce_orders(expert_bits, dp_bits):
    far = [("expert", b) for b in range(2, expert_bits)]
    mid = [("expert", 1)]
    near = [("expert", 0)]
    across = [("dp", b) for b in range(dp_bits - 1, -1, -1)]
    return (near + across + mid + far, near + mid + across + far)


def reduce_shapes(order, expert_bits, dp_bits, rows, width):
    left_e, left_d = expert_bits, dp_bits
    shapes = []
    for axis, _ in order:
        if axis == "expert":
            left_e -= 1
        else:
            left_d -= 1
        shapes.append((2,) * left_e + (rows, width * 2**left_d))
    return shapes


def exchange_kernel(
    n_expert, n_dp, chunks, match, packed, g_back, u_back, w_gate, w_up, landed, result, *scratch
):
    e = lax.axis_index("expert")
    d = lax.axis_index("dp")
    expert_bits, dp_bits = bit_count(n_expert), bit_count(n_dp)
    steps = expert_bits + dp_bits
    halves = 2
    sums = [scratch[i * steps : (i + 1) * steps] for i in range(halves)]
    came = [scratch[(halves + i) * steps : (halves + i + 1) * steps] for i in range(halves)]
    rest = scratch[2 * halves * steps :]
    arrived = rest[:chunks]
    part, ordered, send1, recv1, send2, recv2, own, rsend, rrecv = rest[chunks:]
    size = packed.shape[1] // chunks
    width = result.shape[1]
    half = result.shape[0] // halves

    def peer(axis, bit):
        if axis == "expert":
            return (d, flipped(e, bit))
        return (flipped(d, bit), e)

    barrier = pltpu.get_barrier_semaphore()

    @pl.loop(1, n_expert)
    def _(o):
        pl.semaphore_signal(barrier, inc=1, device_id=(d, (e + o) % n_expert), device_id_type=MESH)

    for b in range(dp_bits):
        pl.semaphore_signal(barrier, inc=1, device_id=(flipped(d, b), e), device_id_type=MESH)

    def rows_of(c):
        return pl.ds(c * size, size)

    stay = [
        pltpu.make_async_copy(packed.at[e, rows_of(c)], arrived[c].at[e], own.at[0, c])
        for c in range(chunks)
    ]
    for c in stay:
        c.start()
    pl.semaphore_wait(barrier, n_expert - 1 + dp_bits)

    def first(c, o):
        to = (e + o) % n_expert
        return pltpu.make_async_remote_copy(
            src_ref=packed.at[to, rows_of(c)],
            dst_ref=arrived[c].at[e],
            send_sem=send1.at[c, o],
            recv_sem=recv1.at[c, o],
            device_id=(d, to),
            device_id_type=MESH,
        )

    def second(c, o):
        return pltpu.make_async_remote_copy(
            src_ref=ordered.at[o, rows_of(c)],
            dst_ref=landed.at[e, rows_of(c)],
            send_sem=send2.at[c, o],
            recv_sem=recv2.at[c, o],
            device_id=(d, (e + o) % n_expert),
            device_id_type=MESH,
        )

    orders = reduce_orders(expert_bits, dp_bits)
    flights = [[], []]

    def split(i, s):
        axis, bit = orders[i][s]
        if s == 0:
            ref, rows = part, pl.ds(i * half, half)
        else:
            ref, rows = sums[i][s - 1], slice(None)
        left = [b for a, b in orders[i][s:] if a == "expert"]
        left = sorted(left, reverse=True)
        if axis == "expert":
            mine = (e // 2**bit) % 2
            at = left.index(bit)

            def where(v):
                return tuple([slice(None)] * at + [v] + [slice(None)] * (len(left) - at - 1)) + (
                    rows,
                    slice(None),
                )

            return ref, where(mine), where(1 - mine)
        mine = (d // 2**bit) % 2
        span = 2**bit * width
        head = (slice(None),) * len(left) + (rows,)
        keep = head + (pl.ds(pl.multiple_of(mine * span, 128), span),)
        give = head + (pl.ds(pl.multiple_of((1 - mine) * span, 128), span),)
        return ref, keep, give

    def start_step(i, s):
        ref, _, give = split(i, s)
        c = pltpu.make_async_remote_copy(
            src_ref=ref.at[give],
            dst_ref=came[i][s],
            send_sem=rsend.at[i, s],
            recv_sem=rrecv.at[i, s],
            device_id=peer(*orders[i][s]),
            device_id_type=MESH,
        )
        c.start()
        flights[i].append(c)

    def end_step(i, s):
        ref, keep, _ = split(i, s)
        flights[i][s].wait_recv()
        total = ref[keep].astype(jnp.float32) + came[i][s][...].astype(jnp.float32)
        sums[i][s][...] = total.astype(sums[i][s].dtype)

    for c in range(chunks):

        @pl.loop(1, n_expert)
        def _(o):
            first(c, o).start()

    model_width = w_gate.shape[0]
    tile = min(512, model_width)
    for t in range(0, model_width, tile):
        piece = lax.dot_general(
            g_back[...], w_gate[t : t + tile], contract_cols, preferred_element_type=jnp.float32
        )
        piece += lax.dot_general(
            u_back[...], w_up[t : t + tile], contract_cols, preferred_element_type=jnp.float32
        )
        shape = part.shape[:-1] + (tile,)
        part[..., t : t + tile] = piece.astype(part.dtype).reshape(shape)
    for i in range(halves):
        start_step(i, 0)

    early = steps - 2
    for s in range(early):
        for i in range(halves):
            end_step(i, s)
            start_step(i, s + 1)
    for c in range(chunks):
        stay[c].wait()

        @pl.loop(1, n_expert)
        def _(o):
            first(c, o).wait_recv()

        @pl.loop(0, n_expert)
        def _(o):
            source = match[(e + o) % n_expert]
            ordered[o, rows_of(c), :] = arrived[c][source]

        pltpu.make_async_copy(
            ordered.at[0, rows_of(c)], landed.at[e, rows_of(c)], own.at[1, c]
        ).start()
        if c == chunks - 1:
            for i in range(halves):
                end_step(i, early)
                start_step(i, early + 1)

        @pl.loop(1, n_expert)
        def _(o):
            second(c, o).start()

    for i in range(halves):
        end_step(i, steps - 1)
    for i in range(halves):
        result[pl.ds(i * half, half), :] = sums[i][steps - 1][...]
    for c in range(chunks):
        pltpu.make_async_copy(
            ordered.at[0, rows_of(c)], landed.at[e, rows_of(c)], own.at[1, c]
        ).wait()

        @pl.loop(1, n_expert)
        def _(o):
            second(c, o).wait_recv()
            first(c, o).wait_send()
            second(c, o).wait_send()

    for f in flights:
        for c in f:
            c.wait_send()


def exchange(n_expert, n_dp, matching, packed, g_back, u_back, w_gate, w_up, tok_rows, width):
    expert_bits, dp_bits = bit_count(n_expert), bit_count(n_dp)
    steps = expert_bits + dp_bits
    chunks = 2 if packed.shape[1] % 32 == 0 else 1
    buffers = []
    for order in reduce_orders(expert_bits, dp_bits):
        for shape in reduce_shapes(order, expert_bits, dp_bits, tok_rows // 2, width):
            buffers.append(pltpu.VMEM(shape, packed.dtype))
    return pl.pallas_call(
        functools.partial(exchange_kernel, n_expert, n_dp, chunks),
        out_shape=(
            jax.ShapeDtypeStruct(packed.shape, packed.dtype),
            jax.ShapeDtypeStruct((tok_rows, width), packed.dtype),
        ),
        in_specs=[
            pl.BlockSpec(memory_space=pltpu.SMEM),
        ]
        + [pl.BlockSpec(memory_space=pltpu.VMEM)] * 5,
        out_specs=[pl.BlockSpec(memory_space=pltpu.VMEM)] * 2,
        scratch_shapes=buffers
        + buffers
        + [pltpu.VMEM((n_expert, packed.shape[1] // chunks, packed.shape[2]), packed.dtype)] * chunks
        + [
            pltpu.VMEM((2,) * expert_bits + (tok_rows, w_gate.shape[0]), packed.dtype),
            pltpu.VMEM(packed.shape, packed.dtype),
            pltpu.SemaphoreType.DMA((chunks, n_expert)),
            pltpu.SemaphoreType.DMA((chunks, n_expert)),
            pltpu.SemaphoreType.DMA((chunks, n_expert)),
            pltpu.SemaphoreType.DMA((chunks, n_expert)),
            pltpu.SemaphoreType.DMA((2, chunks)),
            pltpu.SemaphoreType.DMA((2, steps)),
            pltpu.SemaphoreType.DMA((2, steps)),
        ],
        compiler_params=pltpu.CompilerParams(collective_id=1, has_side_effects=True),
    )(matching, packed, g_back, u_back, w_gate, w_up)


def column(table, index):
    lanes = lax.broadcasted_iota(jnp.int32, table.shape, 1)
    return jnp.sum(jnp.where(lanes == index, table, 0.0), axis=1)


def scaled(cotangent, weight):
    return (cotangent.astype(jnp.float32) * weight[:, None]).astype(jnp.bfloat16)


def selector(weight, blocks, capacity, kinds, slots):
    chosen = (weight > 0.0).reshape(blocks, -1)
    tok_rows = chosen.shape[1]
    at = lax.broadcasted_iota(jnp.int32, (tok_rows, tok_rows), 0)
    to = lax.broadcasted_iota(jnp.int32, (tok_rows, tok_rows), 1)
    upto = jnp.where(at <= to, 1.0, 0.0).astype(jnp.bfloat16)
    rank = jnp.dot(chosen.astype(jnp.bfloat16), upto, preferred_element_type=jnp.float32)
    rank = jnp.where(chosen, rank.astype(jnp.int32) - 1, -1)
    wide = jnp.concatenate([rank] * kinds, axis=1)[:, None, :]
    shape = (blocks, slots, kinds * tok_rows)
    slot = lax.broadcasted_iota(jnp.int32, shape, 1)
    kind = lax.broadcasted_iota(jnp.int32, shape, 2) // tok_rows
    hit = (wide >= 0) & (wide + kind * capacity == slot)
    return jnp.where(hit, 1.0, 0.0).astype(jnp.bfloat16)


def local(n_expert, n_dp, tokens, cotangent, routes, probs, matching, w_gate, w_up, w_down):
    experts = matching.shape[0]
    tok_rows, top_count = routes.shape
    w_gate, w_up, w_down = w_gate[0], w_up[0], w_down[0]
    hidden_width = w_gate.shape[1]
    capacity = max(2, 5 * tok_rows * top_count // (4 * experts))
    slots = -(-3 * capacity // 16) * 16
    me = lax.axis_index("expert")
    lanes = -(-experts // 128) * 128
    names = jnp.arange(lanes, dtype=jnp.int32)
    table = jnp.sum(
        jnp.where(routes[:, :, None] == names[None, None, :], probs[:, :, None], 0.0), axis=1
    )
    rows, cot, table = gather_all(n_expert, n_dp, tokens, cotangent, table)
    weight = column(table, me)
    grads = scaled(cot, weight)
    gate = jnp.dot(rows, w_gate, preferred_element_type=jnp.float32)
    upper = jnp.dot(rows, w_up, preferred_element_type=jnp.float32)
    sig = jax.nn.sigmoid(gate)
    hidden = (gate * sig * upper).astype(jnp.bfloat16)
    hidden_back = jnp.dot(grads, w_down, preferred_element_type=jnp.float32)
    up_back = (hidden_back * gate * sig).astype(jnp.bfloat16)
    gate_back = (hidden_back * upper * sig * (1.0 + gate * (1.0 - sig))).astype(jnp.bfloat16)
    cubes = [v.reshape(experts, tok_rows, hidden_width) for v in (gate_back, up_back, hidden)]
    stacked = jnp.concatenate(cubes, axis=1)
    pick = selector(weight, experts, capacity, 3, slots)
    packed = jnp.einsum(
        "jrt,jth->jrh", pick, stacked, preferred_element_type=jnp.float32
    ).astype(jnp.bfloat16)
    landed, input_grad = exchange(
        n_expert, n_dp, matching, packed, gate_back, up_back, w_gate, w_up, tok_rows, tokens.shape[1]
    )
    partner = jnp.sum(jnp.where(jnp.arange(experts) == me, matching, 0))
    p_weight = column(table, partner)
    p_pick = selector(p_weight, experts, capacity, 3, slots)
    dense = jnp.einsum(
        "jrt,jrh->jth", p_pick, landed, preferred_element_type=jnp.float32
    ).astype(jnp.bfloat16)
    p_grads = scaled(cot, p_weight)
    total = experts * tok_rows

    def take(kind):
        return dense[:, kind * tok_rows : (kind + 1) * tok_rows].reshape(total, hidden_width)

    g_gate = lax.dot_general(rows, take(0), contract_rows, preferred_element_type=jnp.float32)
    g_up = lax.dot_general(rows, take(1), contract_rows, preferred_element_type=jnp.float32)
    g_down = lax.dot_general(p_grads, take(2), contract_rows, preferred_element_type=jnp.float32)
    return (input_grad, g_gate[None], g_up[None], g_down[None])


def solution(mesh):
    weights = P("expert", None, "dp")
    return jax.shard_map(
        functools.partial(local, mesh.shape["expert"], mesh.shape["dp"]),
        mesh=mesh,
        in_specs=(
            P("expert", "dp"),
            P("expert", "dp"),
            P("expert", None),
            P("expert", None),
            P(),
            weights,
            weights,
            weights,
        ),
        out_specs=(P("expert", "dp"), weights, weights, weights),
        check_vma=False,
    )
```

profile of v0, /device:TPU:0, one launch (start us, length us, event | category | flops | bytes accessed | tf_op | source)
XLA Modules:
  0.0 122.7 jit_solution(10914512579275467808)
XLA Ops:
  0.6 1.4 %fusion.39 = s32[]{:T(128)} fusion(s32[16]{0:T(128)} %match.1, s32[]{:T(128)S(6)} %axis_index.12), kind=kLoop, calls=%fused_computation.71 | loop fusion | flops 47 | bytes 72 | tf_op jit(solution)/shard_map/reduce_sum | solution.py:434
  2.1 0.6 iota_compare_fusion.4
  2.8 0.8 copy.14
  3.5 0.8 copy.15
  4.3 0.7 select_reduce_fusion.2.table
  5.1 36.9 %shard_map.111 = (bf16[2,2,2,2,32,2048]{5,4,3,2,1,0:T(8,128)(2,1)}, bf16[2,2,2,2,32,2048]{5,4,3,2,1,0:T(8,128)(2,1)}, f32[2,2,2,2,32,128]{5,4,3,2,1,0:T(8,128)}) custom-call(bf16[32,1024]{1,0:T(8,128)(2,1)} %tokens.1, bf16[32,1024]{1,0:T(8,128)(2,1)} %cotangent.1, f32[32,128]{1,0:T(8,128)} %select_reduce_fusion.2.table), custom_call_target="tpu_custom_call" | custom-call | tf_op jit(solution)/shard_map/pallas_call | solution.py:120
  42.0 1.2 select_reduce_fusion
  43.2 0.1 fusion.16
  43.5 0.1 fusion.14
  43.8 3.6 %fusion.43 = f32[512,512]{1,0:T(8,128)S(1)} fusion(bf16[512,2048]{1,0:T(8,128)(2,1)} %bitcast.47, bf16[1,2048,512]{2,1,0:T(8,128)(2,1)} %param.14), kind=kOutput, calls=%fused_computation.78 | convolution fusion | flops 1073741824 | bytes 5242880 | tf_op jit(solution)/shard_map/dot_general | solution.py:419
  47.4 2.0 %fusion.1 = (bf16[2,2,2,2,32,2048]{5,4,3,2,1,0:T(8,128)(2,1)}, bf16[2,2,2,2,32,2048]{5,4,3,2,1,0:T(8,128)(2,1)S(1)}) fusion(bf16[2,2,2,2,32,2048]{5,4,3,2,1,0:T(8,128)(2,1)S(1)} %copy-done.3, f32[2,2,2,2,32]{4,3,2,1,0:T(2,128)S(1)} %get-tuple-element.14, f32[2,2,2,2,32]{4,3,2,1,0:T(2,128)S(1)} %get-tuple-element.15), kind=kLoop, calls=%fused_computation.3 | loop fusion | flops 5242880 | bytes 6295552 | tf_op jit(solution)/shard_map/convert_element_type | solution.py:383
  49.5 1.2 %fusion.2 = f32[512,512]{1,0:T(8,128)S(1)} fusion(bf16[512,2048]{1,0:T(8,128)(2,1)S(1)} %bitcast.41, bf16[1,2048,512]{2,1,0:T(8,128)(2,1)S(1)} %copy-done), kind=kOutput, calls=%fused_computation.7 | convolution fusion | flops 1073741824 | bytes 5242880 | tf_op jit(solution)/shard_map/dot_general | solution.py:422
  50.7 0.3 copy-done.1
  51.1 0.6 copy-done.7
  51.7 1.7 %multiply_convert_fusion.2 = (bf16[512,512]{1,0:T(8,128)(2,1)S(1)}, bf16[512,512]{1,0:T(8,128)(2,1)S(1)}, bf16[512,512]{1,0:T(8,128)(2,1)S(1)}) fusion(f32[512,512]{1,0:T(8,128)S(1)} %fusion.2, f32[512,512]{1,0:T(8,128)S(1)} %fusion.43, bf16[512,2048]{1,0:T(8,128)(2,1)S(1)} %bitcast.48, bf16[1,2048,512]{2,1,0:T(8,128)(2,1)S(1)} %copy-done.1), kind=kOutput, calls=%fused_computation.25 | convolution fusion | flops 1077936128 | bytes 7864320 | tf_op jit(solution)/shard_map/dot_general | solution.py:418
  53.4 1.4 %fusion.10.packed = bf16[16,64,512]{2,1,0:T(8,128)(2,1)} fusion(bf16[16,32,512]{2,1,0:T(8,128)(2,1)S(1)} %bitcast.51, bf16[16,32,512]{2,1,0:T(8,128)(2,1)S(1)} %bitcast.43, bf16[16,32,512]{2,1,0:T(8,128)(2,1)S(1)} %bitcast.42, s32[96]{0:T(128)S(1)} %get-tuple-element.26, s32[96]{0:T(128)S(1)} %get-tuple-element.27, s32[16,96]{1,0:T(8,128)S(1)} %pad_add_fusion, ...), kind=kOutput, calls=%fused_computation.16 | convolution fusion | flops 106594304 | bytes 2629984 | tf_op jit(solution)/shard_map/jrt,jth->jrh/dot_general | solution.py:428
  54.8 53.8 %shard_map.112 = (bf16[16,64,512]{2,1,0:T(8,128)(2,1)}, bf16[32,1024]{1,0:T(8,128)(2,1)}) custom-call(s32[16]{0:T(128)} %match.1, bf16[16,64,512]{2,1,0:T(8,128)(2,1)} %fusion.10.packed, bf16[512,512]{1,0:T(8,128)(2,1)} %copy-done.4, bf16[512,512]{1,0:T(8,128)(2,1)} %copy-done.5, bf16[2048,512]{1,0:T(8,128)(2,1)} %bitcast.39, bf16[2048,512]{1,0:T(8,128)(2,1)} %bitcast.38), custom_call_target="tpu_custom_call" | custom-call | tf_op jit(solution)/shard_map/pallas_call | solution.py:348
  108.6 1.9 %convolution_convert_fusion = bf16[16,96,512]{2,1,0:T(8,128)(2,1)S(1)} fusion(bf16[16,64,512]{2,1,0:T(8,128)(2,1)} %get-tuple-element.13, s32[16,96]{1,0:T(8,128)S(1)} %pad_add_fusion.1, s32[96]{0:T(128)S(1)} %get-tuple-element.26, s32[96]{0:T(128)S(1)} %get-tuple-element.27, pred[16,96]{1,0:T(8,128)(4,1)S(1)} %broadcast_compare_fusion, ...), kind=kOutput, calls=%fused_computation.9 | convolution fusion | flops 102137856 | bytes 2629984 | tf_op jit(solution)/shard_map/jrt,jrh->jth/dot_general | solution.py:437
  110.5 0.2 fusion.55
  110.7 1.4 %copy-done.2 = bf16[2,2,2,2,32,2048]{5,4,3,2,1,0:T(8,128)(2,1)S(1)} copy-done((bf16[2,2,2,2,32,2048]{5,4,3,2,1,0:T(8,128)(2,1)S(1)}, bf16[2,2,2,2,32,2048]{5,4,3,2,1,0:T(8,128)(2,1)}, u32[]{:S(2)}) %copy-start.2) | copy-done | bytes 2097176
  112.1 3.3 %convolution_bitcast_fusion = f32[1,2048,512]{2,1,0:T(8,128)} fusion(bf16[512,2048]{1,0:T(8,128)(2,1)S(1)} %bitcast.40, bf16[512,512]{1,0:T(8,128)(2,1)S(1)} %bitcast.46), kind=kOutput, calls=%fused_computation.4 | convolution fusion | flops 1073741824 | bytes 6815744 | tf_op jit(solution)/shard_map/dot_general | solution.py:448
  115.4 3.3 %convolution_bitcast_fusion.1 = f32[1,2048,512]{2,1,0:T(8,128)} fusion(bf16[512,2048]{1,0:T(8,128)(2,1)S(1)} %bitcast.49, bf16[512,512]{1,0:T(8,128)(2,1)S(1)} %bitcast.45), kind=kOutput, calls=%fused_computation.5 | convolution fusion | flops 1073741824 | bytes 6815744 | tf_op jit(solution)/shard_map/dot_general | solution.py:447
  118.7 3.3 %convolution_bitcast_fusion.2 = f32[1,2048,512]{2,1,0:T(8,128)} fusion(bf16[512,2048]{1,0:T(8,128)(2,1)S(1)} %bitcast.50, bf16[512,512]{1,0:T(8,128)(2,1)S(1)} %bitcast.44), kind=kOutput, calls=%fused_computation.6 | convolution fusion | flops 1073741824 | bytes 6815744 | tf_op jit(solution)/shard_map/dot_general | solution.py:446
  122.0 0.6 copy.17
  (25 shorter events, 0.4 us)
Async XLA Ops:
  0.6 48.8 %copy-start = (bf16[1,2048,512]{2,1,0:T(8,128)(2,1)S(1)}, bf16[1,2048,512]{2,1,0:T(8,128)(2,1)}, u32[]{:S(2)}) copy-start(bf16[1,2048,512]{2,1,0:T(8,128)(2,1)} %param.15) | copy-start | bytes 6291460
  43.8 3.6 %copy-start.3 = (bf16[2,2,2,2,32,2048]{5,4,3,2,1,0:T(8,128)(2,1)S(1)}, bf16[2,2,2,2,32,2048]{5,4,3,2,1,0:T(8,128)(2,1)}, u32[]{:S(2)}) copy-start(bf16[2,2,2,2,32,2048]{5,4,3,2,1,0:T(8,128)(2,1)} %get-tuple-element.10) | copy-start | bytes 6291460
  49.5 1.6 %copy-start.1 = (bf16[1,2048,512]{2,1,0:T(8,128)(2,1)S(1)}, bf16[1,2048,512]{2,1,0:T(8,128)(2,1)}, u32[]{:S(2)}) copy-start(bf16[1,2048,512]{2,1,0:T(8,128)(2,1)} %param.13) | copy-start | bytes 6291460
  49.5 2.2 %copy-start.7 = (bf16[2,2,2,2,32,2048]{5,4,3,2,1,0:T(8,128)(2,1)S(1)}, bf16[2,2,2,2,32,2048]{5,4,3,2,1,0:T(8,128)(2,1)}, u32[]{:S(2)}) copy-start(bf16[2,2,2,2,32,2048]{5,4,3,2,1,0:T(8,128)(2,1)} %get-tuple-element.11) | copy-start | bytes 6291460
  53.4 1.4 %copy-start.4 = (bf16[512,512]{1,0:T(8,128)(2,1)}, bf16[512,512]{1,0:T(8,128)(2,1)S(1)}, u32[]{:S(2)}) copy-start(bf16[512,512]{1,0:T(8,128)(2,1)S(1)} %get-tuple-element.18.g_back) | copy-start | bytes 1572868
  53.4 1.4 %copy-start.5 = (bf16[512,512]{1,0:T(8,128)(2,1)}, bf16[512,512]{1,0:T(8,128)(2,1)S(1)}, u32[]{:S(2)}) copy-start(bf16[512,512]{1,0:T(8,128)(2,1)S(1)} %get-tuple-element.19.u_back) | copy-start | bytes 1572868
  110.5 1.6 %copy-start.2 = (bf16[2,2,2,2,32,2048]{5,4,3,2,1,0:T(8,128)(2,1)S(1)}, bf16[2,2,2,2,32,2048]{5,4,3,2,1,0:T(8,128)(2,1)}, u32[]{:S(2)}) copy-start(bf16[2,2,2,2,32,2048]{5,4,3,2,1,0:T(8,128)(2,1)} %get-tuple-element.16) | copy-start | bytes 6291460
  112.1 3.3 %copy-start.8 = (bf16[2,2,2,2,32,2048]{5,4,3,2,1,0:T(8,128)(2,1)S(1)}, bf16[2,2,2,2,32,2048]{5,4,3,2,1,0:T(8,128)(2,1)}, u32[]{:S(2)}) copy-start(bf16[2,2,2,2,32,2048]{5,4,3,2,1,0:T(8,128)(2,1)} %get-tuple-element.11) | copy-start | bytes 6291460
  118.7 3.3 %copy-start.6 = (bf16[32,1024]{1,0:T(8,128)(2,1)S(1)}, bf16[32,1024]{1,0:T(8,128)(2,1)}, u32[]{:S(2)}) copy-start(bf16[32,1024]{1,0:T(8,128)(2,1)} %get-tuple-element.32) | copy-start | bytes 196612
where the time goes:
time: 124 us; the launch traced here: 123 us
  Pallas kernels  90.7 us (73%)
  matrix products  20 us (16%)
  other arithmetic  6.4 us (5%)
  local copies, waits for them, and re-layouts  4.78 us (4%)
    pallas_call x1, Pallas kernels, exchange(): pl.pallas_call(functools.partial(exchange_kernel, n_expert, n_dp, chunks)...  53.8 us
    pallas_call x1, Pallas kernels, gather_all(): pl.pallas_call(functools.partial(gather_kernel, n_expert, n_dp), out_shap...  36.9 us
    unnamed x21, local copies, waits for them, and re-layouts  4.57 us
    dot_general x1, matrix products, local(): upper = jnp.dot(rows, w_up, preferred_element_type=jnp.float32)  3.62 us
    dot_general x1, matrix products, local(): lax.dot_general(rows, take(0), contract_rows, preferred_element_type=jnp....  3.32 us
    dot_general x1, matrix products, local(): lax.dot_general(rows, take(1), contract_rows, preferred_element_type=jnp....  3.32 us
    dot_general x1, matrix products, local(): lax.dot_general(p_grads, take(2), contract_rows, preferred_element_type=j...  3.32 us

commit v1 on v0

v1 whole, which is shorter than its diff:
```python
import functools
import math

import jax
import jax.numpy as jnp
from jax import lax
from jax.experimental import pallas as pl
from jax.experimental.pallas import tpu as pltpu
from jax.sharding import PartitionSpec as P

contract_rows = (((0,), (0,)), ((), ()))
contract_cols = (((1,), (1,)), ((), ()))
MESH = pl.DeviceIdType.MESH
KINDS = 3
LANES = 128
CHUNKS = 2


def bit_count(size):
    return size.bit_length() - 1


def flipped(index, bit):
    step = 2**bit
    return index + step * (1 - 2 * ((index // step) % 2))


def gather_orders(expert_bits, dp_bits):
    far = [("expert", b) for b in range(expert_bits - 1, 1, -1)]
    mid = [("expert", 1)]
    last = [("expert", 0)]
    across = [("dp", b) for b in range(dp_bits)]
    return (
        far + across + mid + last,
        across + far + mid + last,
        far + mid + across + last,
        mid + far + across + last,
        far + mid + last,
    )


def reduce_orders(expert_bits, dp_bits):
    far = [("expert", b) for b in range(2, expert_bits)]
    mid = [("expert", 1)]
    near = [("expert", 0)]
    across = [("dp", b) for b in range(dp_bits - 1, -1, -1)]
    return (near + across + mid + far, near + mid + across + far)


def reduce_shapes(order, expert_bits, dp_bits, rows, width):
    left_e, left_d = expert_bits, dp_bits
    shapes = []
    for axis, _ in order:
        if axis == "expert":
            left_e -= 1
        else:
            left_d -= 1
        shapes.append((2,) * left_e + (rows, width * 2**left_d))
    return shapes


class Plan:
    def __init__(self, n_expert, n_dp, tok_rows, width, top_count, hidden):
        self.n_expert, self.n_dp = n_expert, n_dp
        self.expert_bits, self.dp_bits = bit_count(n_expert), bit_count(n_dp)
        self.tok_rows, self.width, self.hidden = tok_rows, width, hidden
        self.top_count = top_count
        self.model = width * n_dp
        self.total = n_expert * tok_rows
        self.capacity = max(2, 5 * tok_rows * top_count // (4 * n_expert))
        self.blocks = 16 // math.gcd(16, self.capacity)
        self.groups = n_expert // self.blocks
        self.group_slots = self.blocks * self.capacity
        self.group_toks = self.blocks * tok_rows
        self.slots = self.groups * self.group_slots
        self.half = n_expert // 2
        self.chunks = CHUNKS
        self.chunk_groups = self.groups // self.chunks
        self.col_tiles = hidden // LANES
        self.row_split = max(1, self.half // (self.chunk_groups * self.col_tiles))
        unit = 16 * self.row_split
        self.group_rows = -(-KINDS * self.group_slots // unit) * unit
        self.piece_rows = self.group_rows // self.row_split
        self.chunk_toks = self.total // self.chunks
        self.steps = self.expert_bits + self.dp_bits
        self.row_parts = 2 if 2**self.steps <= 128 else 1


def comm_kernel(
    p,
    crossing,
    match,
    tokens,
    cotangent,
    routes,
    probs,
    h_gate,
    h_up,
    h_down,
    landed,
    out_rows,
    out_grads,
    result,
    *scratch,
):
    n, half = p.n_expert, p.half
    steps, chunks = p.steps, p.chunks
    halves = 2
    sums = [scratch[i * steps : (i + 1) * steps] for i in range(halves)]
    came = [scratch[(halves + i) * steps : (halves + i + 1) * steps] for i in range(halves)]
    rest = scratch[2 * halves * steps :]
    arrived = rest[:chunks]
    swapped = rest[chunks : 2 * chunks]
    staged = rest[2 * chunks : 3 * chunks]
    ordered = rest[3 * chunks : 4 * chunks]
    (
        all_tok,
        all_cot,
        all_routes,
        all_probs,
        w_gate,
        w_up,
        w_down,
        weights,
        places,
        p_weights,
        p_places,
        scaled,
        backs,
        packed,
        part,
        x_rows,
        x_grads,
        summed,
        gsend,
        grecv,
        msend,
        mrecv,
        own,
        wsem,
        send1,
        recv1,
        send2,
        recv2,
        send3,
        recv3,
        stay1,
        stay3,
        rsend,
        rrecv,
        osem,
    ) = rest[4 * chunks :]
    e = lax.axis_index("expert")
    d = lax.axis_index("dp")
    h = e % half
    base = e - h
    rows_half = p.tok_rows // 2
    part_rows = p.tok_rows // p.row_parts
    width = p.width

    def peer(axis, bit):
        if axis == "expert":
            return (d, flipped(e, bit))
        return (flipped(d, bit), e)

    def origin(order, mask):
        at_e, at_d = e, d
        for k, (axis, bit) in enumerate(order):
            if mask >> k & 1:
                if axis == "expert":
                    at_e = flipped(at_e, bit)
                else:
                    at_d = flipped(at_d, bit)
        return at_e, at_d

    orders = gather_orders(p.expert_bits, p.dp_bits)
    sources = (
        (tokens, all_tok, 0, orders[0]),
        (cotangent, all_cot, 0, orders[1]),
        (tokens, all_tok, 1, orders[2]),
        (cotangent, all_cot, 1, orders[3]),
    )[: 2 * p.row_parts]

    def block(dst, index, at_e, at_d):
        row = pl.multiple_of(at_e * p.tok_rows + index * part_rows, part_rows)
        col = pl.multiple_of(at_d * width, width)
        return dst.at[pl.ds(row, part_rows), pl.ds(col, width)]

    metas = ((routes, all_routes), (probs, all_probs))
    locals_ = []
    for i, (src, dst) in enumerate(((tokens, all_tok), (cotangent, all_cot))):
        row = pl.multiple_of(e * p.tok_rows, p.tok_rows)
        col = pl.multiple_of(d * width, width)
        c = pltpu.make_async_copy(
            src, dst.at[pl.ds(row, p.tok_rows), pl.ds(col, width)], own.at[i]
        )
        c.start()
        locals_.append(c)
    for i, (src, dst) in enumerate(metas):
        c = pltpu.make_async_copy(src, dst.at[e], own.at[2 + i])
        c.start()
        locals_.append(c)

    barrier = pltpu.get_barrier_semaphore()

    @pl.loop(1, half)
    def _(o):
        pl.semaphore_signal(
            barrier, inc=1, device_id=(d, base + (h + o) % half), device_id_type=MESH
        )

    mirror = (d, (e + half) % n)
    pl.semaphore_signal(barrier, inc=1, device_id=mirror, device_id_type=MESH)
    for b in range(p.dp_bits):
        pl.semaphore_signal(barrier, inc=1, device_id=(flipped(d, b), e), device_id_type=MESH)
    pl.semaphore_wait(barrier, half + p.dp_bits)

    def flight(i, mask, k):
        src, dst, index, order = sources[i]
        at = block(dst, index, *origin(order, mask))
        if mask == 0:
            src = src.at[pl.ds(index * part_rows, part_rows)]
        else:
            src = at
        got = mask + 2**k
        return pltpu.make_async_remote_copy(
            src_ref=src,
            dst_ref=at,
            send_sem=gsend.at[i, got],
            recv_sem=grecv.at[i, got],
            device_id=peer(*order[k]),
            device_id_type=MESH,
        )

    def meta_flight(i, mask, k):
        src, dst = metas[i]
        at = dst.at[origin(orders[4], mask)[0]]
        got = mask + 2**k
        return pltpu.make_async_remote_copy(
            src_ref=src if mask == 0 else at,
            dst_ref=at,
            send_sem=msend.at[i, got],
            recv_sem=mrecv.at[i, got],
            device_id=peer(*orders[4][k]),
            device_id_type=MESH,
        )

    flights, meta_flights = {}, {}

    def send_on(i, mask):
        top = mask.bit_length()
        for k in range(top, steps):
            c = flight(i, mask, k)
            c.start()
            flights[i, mask + 2**k] = c

    def meta_on(i, mask):
        for k in range(mask.bit_length(), p.expert_bits):
            c = meta_flight(i, mask, k)
            c.start()
            meta_flights[i, mask + 2**k] = c

    for i in range(len(sources)):
        send_on(i, 0)
    for i in range(len(metas)):
        meta_on(i, 0)
    loads = []
    for i, (src, dst) in enumerate(((h_gate, w_gate), (h_up, w_up), (h_down, w_down))):
        c = pltpu.make_async_copy(src, dst, wsem.at[i])
        c.start()
        loads.append(c)

    def turn(mask):
        top = 2 ** (mask.bit_length() - 1)
        return (mask - top, top)

    inner = sorted(range(1, 2 ** (steps - 1)), key=turn)
    meta_masks = sorted(range(1, 2**p.expert_bits), key=turn)
    for count, mask in enumerate(inner):
        for i in range(len(sources)):
            flights[i, mask].wait_recv()
            send_on(i, mask)
        if count < len(meta_masks):
            for i in range(len(metas)):
                meta_flights[i, meta_masks[count]].wait_recv()
                meta_on(i, meta_masks[count])
    for mask in meta_masks[len(inner) :]:
        for i in range(len(metas)):
            meta_flights[i, mask].wait_recv()
            meta_on(i, mask)
    for c in locals_:
        c.wait()

    partner = match[e]
    tok = p.tok_rows
    at = lax.broadcasted_iota(jnp.int32, (tok, tok), 0)
    to = lax.broadcasted_iota(jnp.int32, (tok, tok), 1)

    @pl.loop(0, n)
    def _(b):
        r = all_routes[b]
        q = all_probs[b]
        rows = pl.ds(pl.multiple_of(b * tok, tok), tok)
        start = ((b % p.blocks) * p.capacity).astype(jnp.float32)
        for who, w_ref, s_ref in ((e, weights, places), (partner, p_weights, p_places)):
            hit = r == who
            w = jnp.sum(jnp.where(hit, q, 0.0), axis=0, keepdims=True)
            f = jnp.sum(jnp.where(hit, 1.0, 0.0), axis=0, keepdims=True)
            w = jnp.broadcast_to(w, (tok, tok))
            f = jnp.broadcast_to(f, (tok, tok))
            w_col = jnp.sum(jnp.where(at == to, w, 0.0), axis=1, keepdims=True)
            f_col = jnp.sum(jnp.where(at == to, f, 0.0), axis=1, keepdims=True)
            rank = jnp.sum(jnp.where(to < at, f, 0.0), axis=1, keepdims=True)
            s_col = jnp.where(f_col > 0.5, rank + start, -1.0)
            w_ref[rows, :] = jnp.broadcast_to(w_col, (tok, LANES))
            s_ref[rows, :] = jnp.broadcast_to(s_col, (tok, LANES))

    def picker(s_ref, g):
        place = s_ref[g * p.group_toks : (g + 1) * p.group_toks, :]
        lane = lax.broadcasted_iota(jnp.int32, place.shape, 1).astype(jnp.float32)
        hot = jnp.where(place == lane, 1.0, 0.0)
        return jnp.transpose(hot)[: p.group_slots].astype(jnp.bfloat16)

    for mask in range(2 ** (steps - 1), 2**steps):
        for i in range(len(sources)):
            flights[i, mask].wait_recv()
    for c in loads:
        c.wait()

    tile_rows = min(256, p.chunk_toks)
    tile_cols = min(256, p.hidden)

    def forward(c):
        @pl.loop(0, p.chunk_toks // tile_rows)
        def _(t):
            first_row = pl.multiple_of(c * p.chunk_toks + t * tile_rows, tile_rows)
            rows = pl.ds(first_row, tile_rows)
            w = weights[rows, :][:, :1]
            scaled[...] = (all_cot[rows, :].astype(jnp.float32) * w).astype(jnp.bfloat16)

            @pl.loop(0, p.hidden // tile_cols)
            def _(u):
                cols = pl.ds(pl.multiple_of(u * tile_cols, tile_cols), tile_cols)
                x = all_tok[rows, :]
                gate = jnp.dot(x, w_gate[0, :, cols], preferred_element_type=jnp.float32)
                upper = jnp.dot(x, w_up[0, :, cols], preferred_element_type=jnp.float32)
                back = jnp.dot(
                    scaled[...], w_down[0, :, cols], preferred_element_type=jnp.float32
                )
                sig = jax.nn.sigmoid(gate)
                backs[0, rows, cols] = (
                    back * upper * sig * (1.0 + gate * (1.0 - sig))
                ).astype(jnp.bfloat16)
                backs[1, rows, cols] = (back * gate * sig).astype(jnp.bfloat16)
                backs[2, rows, cols] = (gate * sig * upper).astype(jnp.bfloat16)

    def pack(c):
        for gl in range(p.chunk_groups):
            g = c * p.chunk_groups + gl
            pick = picker(places, g)
            rows = slice(g * p.group_toks, (g + 1) * p.group_toks)
            kinds = [
                jnp.dot(pick, backs[k, rows, :], preferred_element_type=jnp.float32).astype(
                    jnp.bfloat16
                )
                for k in range(KINDS)
            ]
            spare = p.group_rows - KINDS * p.group_slots
            if spare:
                kinds.append(jnp.zeros((spare, p.hidden), jnp.bfloat16))
            whole = jnp.concatenate(kinds, axis=0)
            for t in range(p.col_tiles):
                j = (gl * p.col_tiles + t) * p.row_split
                piece = whole[:, t * LANES : (t + 1) * LANES]
                packed[c, j : j + p.row_split] = piece.reshape(
                    p.row_split, p.piece_rows, LANES
                )

    def spread(c, o):
        to_h = (h + o) % half
        return pltpu.make_async_remote_copy(
            src_ref=packed.at[c, to_h],
            dst_ref=arrived[c].at[h],
            send_sem=send1.at[c, o],
            recv_sem=recv1.at[c, o],
            device_id=(d, base + to_h),
            device_id_type=MESH,
        )

    def swap(c):
        return pltpu.make_async_remote_copy(
            src_ref=staged[c],
            dst_ref=swapped[c],
            send_sem=send2.at[c],
            recv_sem=recv2.at[c],
            device_id=mirror,
            device_id_type=MESH,
        )

    def collect(c, o):
        to_h = (h + o) % half
        return pltpu.make_async_remote_copy(
            src_ref=ordered[c].at[to_h],
            dst_ref=landed.at[c, h],
            send_sem=send3.at[c, o],
            recv_sem=recv3.at[c, o],
            device_id=(d, base + to_h),
            device_id_type=MESH,
        )

    def stay_first(c):
        return pltpu.make_async_copy(packed.at[c, h], arrived[c].at[h], stay1.at[c])

    def stay_last(c):
        return pltpu.make_async_copy(ordered[c].at[h], landed.at[c, h], stay3.at[c])

    def begin(c):
        forward(c)
        pack(c)
        stay_first(c).start()

        @pl.loop(1, half)
        def _(o):
            spread(c, o).start()

    def cross_list(start):
        flags, before, count = [], [], 0
        for i in range(half):
            m = match[start + i]
            inside = (m >= start) & (m < start + half)
            flag = jnp.where(inside, 0, 1)
            flags.append(flag)
            before.append(count)
            count = count + flag
        return flags, before

    def cross_at(listed, k):
        flags, before = listed
        found = 0
        for i in range(half):
            found = found + jnp.where((flags[i] == 1) & (before[i] == k), i, 0)
        return found

    other = (base + half) % n
    full = crossing == half

    def swap_on(c):
        stay_first(c).wait()

        @pl.loop(1, half)
        def _(o):
            spread(c, o).wait_recv()

        if full:
            staged[c][...] = arrived[c][...]
        else:
            mine = cross_list(base)
            for k in range(crossing):
                staged[c][k] = arrived[c][cross_at(mine, k)]
        swap(c).start()

    def collect_on(c):
        swap(c).wait_recv()
        theirs = None if full else cross_list(other)
        for i in range(half):
            m = match[base + i]
            inside = (m >= base) & (m < base + half)
            near = arrived[c][jnp.where(inside, m - base, 0)]
            if full:
                far_at = jnp.where(inside, 0, m - other)
            else:
                far_at = 0
                for k in range(half):
                    far_at = far_at + jnp.where(m - other == k, theirs[1][k], 0)
                far_at = jnp.where(inside, 0, far_at)
            far = swapped[c][far_at]
            ordered[c][i] = jnp.where(inside, near, far)
        stay_last(c).start()

        @pl.loop(1, half)
        def _(o):
            collect(c, o).start()

    r_orders = reduce_orders(p.expert_bits, p.dp_bits)
    r_flights = [[], []]

    def split(i, s):
        axis, bit = r_orders[i][s]
        if s == 0:
            ref, rows = part, pl.ds(i * rows_half, rows_half)
        else:
            ref, rows = sums[i][s - 1], slice(None)
        left = [b for a, b in r_orders[i][s:] if a == "expert"]
        left = sorted(left, reverse=True)
        if axis == "expert":
            mine = (e // 2**bit) % 2
            spot = left.index(bit)

            def where(v):
                return tuple(
                    [slice(None)] * spot + [v] + [slice(None)] * (len(left) - spot - 1)
                ) + (rows, slice(None))

            return ref, where(mine), where(1 - mine)
        mine = (d // 2**bit) % 2
        span = 2**bit * width
        head = (slice(None),) * len(left) + (rows,)
        keep = head + (pl.ds(pl.multiple_of(mine * span, LANES), span),)
        give = head + (pl.ds(pl.multiple_of((1 - mine) * span, LANES), span),)
        return ref, keep, give

    def start_step(i, s):
        ref, _, give = split(i, s)
        c = pltpu.make_async_remote_copy(
            src_ref=ref.at[give],
            dst_ref=came[i][s],
            send_sem=rsend.at[i, s],
            recv_sem=rrecv.at[i, s],
            device_id=peer(*r_orders[i][s]),
            device_id_type=MESH,
        )
        c.start()
        r_flights[i].append(c)

    def end_step(i, s):
        ref, keep, _ = split(i, s)
        r_flights[i][s].wait_recv()
        total = ref[keep].astype(jnp.float32) + came[i][s][...].astype(jnp.float32)
        sums[i][s][...] = total.astype(sums[i][s].dtype)

    def next_step(s):
        for i in range(halves):
            end_step(i, s)
            if s + 1 < steps:
                start_step(i, s + 1)

    def pack_rows(src, dst, w_ref):
        for g in range(p.groups):
            pick = picker(p_places, g)
            rows = slice(g * p.group_toks, (g + 1) * p.group_toks)
            at_rows = slice(g * p.group_slots, (g + 1) * p.group_slots)
            span = min(512, p.model)
            for t in range(0, p.model, span):
                x = src[rows, t : t + span]
                if w_ref is not None:
                    x = (x.astype(jnp.float32) * w_ref[rows, :][:, :1]).astype(jnp.bfloat16)
                dst[at_rows, t : t + span] = jnp.dot(
                    pick, x, preferred_element_type=jnp.float32
                ).astype(jnp.bfloat16)

    for c in range(chunks):
        begin(c)
    swap_on(0)
    tile = min(512, p.model)
    for t in range(0, p.model, tile):
        piece = lax.dot_general(
            backs[0], w_gate[0, t : t + tile], contract_cols, preferred_element_type=jnp.float32
        )
        piece += lax.dot_general(
            backs[1], w_up[0, t : t + tile], contract_cols, preferred_element_type=jnp.float32
        )
        shape = part.shape[:-1] + (tile,)
        part[..., t : t + tile] = piece.astype(part.dtype).reshape(shape)
    for i in range(halves):
        start_step(i, 0)
    for c in range(1, chunks):
        swap_on(c)
    pack_rows(all_tok, x_rows, None)
    row_out = pltpu.make_async_copy(x_rows, out_rows, osem.at[0])
    row_out.start()
    next_step(0)
    pack_rows(all_cot, x_grads, p_weights)
    grad_out = pltpu.make_async_copy(x_grads, out_grads, osem.at[1])
    grad_out.start()
    next_step(1)
    collect_on(0)
    for s in range(2, steps - 1):
        next_step(s)
    for c in range(1, chunks):
        collect_on(c)
    next_step(steps - 1)
    for i in range(halves):
        summed[pl.ds(i * rows_half, rows_half), :] = sums[i][steps - 1][...]
    result_out = pltpu.make_async_copy(summed, result, osem.at[2])
    result_out.start()

    for c in flights.values():
        c.wait_send()
    for c in meta_flights.values():
        c.wait_send()
    for f in r_flights:
        for c in f:
            c.wait_send()
    row_out.wait()
    grad_out.wait()
    result_out.wait()
    for c in range(chunks):
        stay_last(c).wait()
        swap(c).wait_send()

        @pl.loop(1, half)
        def _(o):
            spread(c, o).wait_send()
            collect(c, o).wait_send()
            collect(c, o).wait_recv()


def communicate(p, crossing, call_id, operands):
    dtype = operands[1].dtype
    reduce_buffers = []
    for order in reduce_orders(p.expert_bits, p.dp_bits):
        for shape in reduce_shapes(order, p.expert_bits, p.dp_bits, p.tok_rows // 2, p.width):
            reduce_buffers.append(pltpu.VMEM(shape, dtype))
    piece = (p.piece_rows, LANES)
    weight = operands[-1].shape
    dma = pltpu.SemaphoreType.DMA
    steps, chunks, half = p.steps, p.chunks, p.half
    scratch = (
        reduce_buffers
        + reduce_buffers
        + [pltpu.VMEM((half,) + piece, dtype)] * chunks
        + [pltpu.VMEM((crossing,) + piece, dtype)] * (2 * chunks)
        + [pltpu.VMEM((half,) + piece, dtype)] * chunks
        + [
            pltpu.VMEM((p.total, p.model), dtype),
            pltpu.VMEM((p.total, p.model), dtype),
            pltpu.VMEM((p.n_expert, p.top_count, p.tok_rows), jnp.int32),
            pltpu.VMEM((p.n_expert, p.top_count, p.tok_rows), jnp.float32),
            pltpu.VMEM(weight, dtype),
            pltpu.VMEM(weight, dtype),
            pltpu.VMEM(weight, dtype),
            pltpu.VMEM((p.total, LANES), jnp.float32),
            pltpu.VMEM((p.total, LANES), jnp.float32),
            pltpu.VMEM((p.total, LANES), jnp.float32),
            pltpu.VMEM((p.total, LANES), jnp.float32),
            pltpu.VMEM((min(256, p.chunk_toks), p.model), dtype),
            pltpu.VMEM((KINDS, p.total, p.hidden), dtype),
            pltpu.VMEM((chunks, half) + piece, dtype),
            pltpu.VMEM((2,) * p.expert_bits + (p.tok_rows, p.model), dtype),
            pltpu.VMEM((p.slots, p.model), dtype),
            pltpu.VMEM((p.slots, p.model), dtype),
            pltpu.VMEM((p.tok_rows, p.width), dtype),
            dma((2 * p.row_parts, 2**steps)),
            dma((2 * p.row_parts, 2**steps)),
            dma((2, p.n_expert)),
            dma((2, p.n_expert)),
            dma((4,)),
            dma((3,)),
            dma((chunks, half)),
            dma((chunks, half)),
            dma((chunks,)),
            dma((chunks,)),
            dma((chunks, half)),
            dma((chunks, half)),
            dma((chunks,)),
            dma((chunks,)),
            dma((2, steps)),
            dma((2, steps)),
            dma((3,)),
        ]
    )
    anywhere = pl.BlockSpec(memory_space=pl.ANY)
    return pl.pallas_call(
        functools.partial(comm_kernel, p, crossing),
        out_shape=(
            jax.ShapeDtypeStruct((chunks, half) + piece, dtype),
            jax.ShapeDtypeStruct((p.slots, p.model), dtype),
            jax.ShapeDtypeStruct((p.slots, p.model), dtype),
            jax.ShapeDtypeStruct((p.tok_rows, p.width), dtype),
        ),
        in_specs=[pl.BlockSpec(memory_space=pltpu.SMEM)] + [anywhere] * 7,
        out_specs=[anywhere] * 4,
        scratch_shapes=scratch,
        compiler_params=pltpu.CompilerParams(
            collective_id=call_id, has_side_effects=True, vmem_limit_bytes=64 * 2**20 - 2**16
        ),
    )(*operands)


def final_kernel(p, landed, rows, grads, summed, g_gate, g_up, g_down, out, acts):
    @pl.when(pl.program_id(0) == 0)
    def _():
        out[...] = summed[...]
        for c in range(p.chunks):
            for gl in range(p.chunk_groups):
                at = (c * p.chunk_groups + gl) * p.group_slots
                for t in range(p.col_tiles):
                    j = (gl * p.col_tiles + t) * p.row_split
                    piece = landed[c, j : j + p.row_split].reshape(p.group_rows, LANES)
                    for k in range(KINDS):
                        acts[k, at : at + p.group_slots, t * LANES : (t + 1) * LANES] = piece[
                            k * p.group_slots : (k + 1) * p.group_slots
                        ]

    x = rows[...]
    g_gate[0] = lax.dot_general(x, acts[0], contract_rows, preferred_element_type=jnp.float32)
    g_up[0] = lax.dot_general(x, acts[1], contract_rows, preferred_element_type=jnp.float32)
    g_down[0] = lax.dot_general(
        grads[...], acts[2], contract_rows, preferred_element_type=jnp.float32
    )


def finish(p, landed, rows, grads, summed):
    tile = min(256, p.model)
    wide = pl.BlockSpec((p.slots, tile), lambda i: (0, i))
    grad = pl.BlockSpec((1, tile, p.hidden), lambda i: (0, i, 0))
    grad_shape = jax.ShapeDtypeStruct((1, p.model, p.hidden), jnp.float32)
    whole = pl.BlockSpec(landed.shape, lambda i: (0, 0, 0, 0))
    small = pl.BlockSpec(summed.shape, lambda i: (0, 0))
    return pl.pallas_call(
        functools.partial(final_kernel, p),
        out_shape=(
            grad_shape,
            grad_shape,
            grad_shape,
            jax.ShapeDtypeStruct(summed.shape, summed.dtype),
        ),
        grid=(p.model // tile,),
        in_specs=[whole, wide, wide, small],
        out_specs=[grad, grad, grad, small],
        scratch_shapes=[pltpu.VMEM((KINDS, p.slots, p.hidden), landed.dtype)],
    )(landed, rows, grads, summed)


def local(n_expert, n_dp, tokens, cotangent, routes, probs, matching, w_gate, w_up, w_down):
    tok_rows, top_count = routes.shape
    p = Plan(n_expert, n_dp, tok_rows, tokens.shape[1], top_count, w_gate.shape[2])
    operands = (matching, tokens, cotangent, routes.T, probs.T, w_gate, w_up, w_down)
    landed, rows, grads, summed = communicate(p, p.half, 0, operands)
    g_gate, g_up, g_down, input_grad = finish(p, landed, rows, grads, summed)
    return input_grad, g_gate, g_up, g_down


def solution(mesh):
    weights = P("expert", None, "dp")
    return jax.shard_map(
        functools.partial(local, mesh.shape["expert"], mesh.shape["dp"]),
        mesh=mesh,
        in_specs=(
            P("expert", "dp"),
            P("expert", "dp"),
            P("expert", None),
            P("expert", None),
            P(),
            weights,
            weights,
            weights,
        ),
        out_specs=(P("expert", "dp"), weights, weights, weights),
        check_vma=False,
    )
```

time: 124 us -> 105 us (0.85)
  matrix products: 20 us -> 0 us
  Pallas kernels: 90.7 us -> 103 us
  other arithmetic: 6.4 us -> 0 us
  local copies, waits for them, and re-layouts: 4.78 us -> 0 us
    dot_general x10 -> x0, matrix products: 20 us -> none  [the longest x1 3.62 us: local(): upper = jnp.dot(rows, w_up, preferred_element_type=jnp.float32)]
    pallas_call x2, Pallas kernels: 90.7 us -> 103 us  [the longest x1 93.1 us: communicate(): pl.pallas_call(functools.partial(comm_kernel, p, crossing), out_shape=(ja...]
    unnamed x21 -> x0, local copies, waits for them, and re-layouts: 4.57 us -> none
    reduce_sum x3 -> x0, other arithmetic: 3.36 us -> none  [the longest x1 1.44 us: local(): partner = jnp.sum(jnp.where(jnp.arange(experts) == me, matching, 0))]
    convert_element_type x1 -> x0, other arithmetic: 2.04 us -> none  [scaled(): (cotangent.astype(jnp.float32) * weight[:, None]).astype(jnp.bfloat16)]
where the time goes in v1:
time: 105 us; the launch traced here: 103 us
  Pallas kernels  103 us (98%)
    pallas_call x1, Pallas kernels, communicate(): pl.pallas_call(functools.partial(comm_kernel, p, crossing), out_shape=(ja...  93.1 us
    pallas_call x1, Pallas kernels, finish(): pl.pallas_call(functools.partial(final_kernel, p), out_shape=(grad_shape,...  9.73 us

profile of v1, /device:TPU:0, one launch (start us, length us, event | category | flops | bytes accessed | tf_op | source)
XLA Modules:
  0.0 103.5 jit_solution(270044970519687871)
XLA Ops:
  0.6 93.1 %shard_map.111 = (bf16[2,8,240,128]{3,2,1,0:T(8,128)(2,1)}, bf16[320,2048]{1,0:T(8,128)(2,1)}, bf16[320,2048]{1,0:T(8,128)(2,1)}, bf16[32,1024]{1,0:T(8,128)(2,1)}) custom-call(s32[16]{0:T(128)} %match.1, bf16[32,1024]{1,0:T(8,128)(2,1)} %tokens.1, bf16[32,1024]{1,0:T(8,128)(2,1)} %cotangent.1, s32[8,32]{1,0:T(8,128)} %bitcast.2, f32[8,32]{1,0:T(8,128)} %bitcast.3, ...), custom_call_target="tpu_custom_call" | custom-call | tf_op jit(solution)/shard_map/pallas_call | solution.py:663
  93.7 9.7 %shard_map.112 = (f32[1,2048,512]{2,1,0:T(8,128)}, f32[1,2048,512]{2,1,0:T(8,128)}, f32[1,2048,512]{2,1,0:T(8,128)}, bf16[32,1024]{1,0:T(8,128)(2,1)}) custom-call(bf16[2,8,240,128]{3,2,1,0:T(8,128)(2,1)} %get-tuple-element.12.landed, bf16[320,2048]{1,0:T(8,128)(2,1)} %get-tuple-element.13.rows, bf16[320,2048]{1,0:T(8,128)(2,1)} %get-tuple-element.14.grads, ...), custom_call_target="tpu_custom_call" | custom-call | tf_op jit(solution)/shard_map/pallas_call | solution.py:710

commit v2 on v1

--- a/solution.py
+++ b/solution.py
@@ -726,7 +726,14 @@
     tok_rows, top_count = routes.shape
     p = Plan(n_expert, n_dp, tok_rows, tokens.shape[1], top_count, w_gate.shape[2])
     operands = (matching, tokens, cotangent, routes.T, probs.T, w_gate, w_up, w_down)
-    landed, rows, grads, summed = communicate(p, p.half, 0, operands)
+    sizes = (p.half // 2, 3 * p.half // 4, p.half)
+    pairs = jnp.sum((matching[: p.half] >= p.half).astype(jnp.int32))
+    which = sum((pairs > size).astype(jnp.int32) for size in sizes[:-1])
+    calls = [
+        functools.partial(lambda size, i, *a: communicate(p, size, i, a), size, i)
+        for i, size in enumerate(sizes)
+    ]
+    landed, rows, grads, summed = lax.switch(which, calls, *operands)
     g_gate, g_up, g_down, input_grad = finish(p, landed, rows, grads, summed)
     return input_grad, g_gate, g_up, g_down
 

time: 105 us -> 94.7 us (0.902)
  Pallas kernels: 103 us -> 89.7 us
  between operations: 0.64 us -> 1.94 us
  other arithmetic: 0 us -> 1.29 us
    pallas_call x1, Pallas kernels: 93.1 us -> 80 us  [communicate(): pl.pallas_call(functools.partial(comm_kernel, p, crossing), out_shape=(ja...]
    reduce_sum x0 -> x1, other arithmetic: none -> 1.29 us  [local(): pairs = jnp.sum((matching[:p.half] >= p.half).astype(jnp.int32))]
where the time goes in v2:
time: 94.7 us; the launch traced here: 93.2 us
  Pallas kernels  89.7 us (95%)
  between operations  1.94 us (2%)
  other arithmetic  1.29 us (1%)
    pallas_call x1, Pallas kernels, communicate(): pl.pallas_call(functools.partial(comm_kernel, p, crossing), out_shape=(ja...  80 us
    pallas_call x1, Pallas kernels, finish(): pl.pallas_call(functools.partial(final_kernel, p), out_shape=(grad_shape,...  9.73 us

profile of v2, /device:TPU:0, one launch (start us, length us, event | category | flops | bytes accessed | tf_op | source)
XLA Modules:
  0.0 93.2 jit_solution(16553228679896531105)
XLA Ops:
  0.6 1.3 %fusion = s32[]{:T(128)} fusion(s32[16]{0:T(128)} %param.15), kind=kLoop, calls=%fused_computation.1 | loop fusion | flops 23 | bytes 36 | tf_op jit(solution)/shard_map/reduce_sum | solution.py:730
  3.2 80.2 %conditional.1 = ((bf16[2,8,240,128]{3,2,1,0:T(8,128)(2,1)}, bf16[320,2048]{1,0:T(8,128)(2,1)}, bf16[320,2048]{1,0:T(8,128)(2,1)}, bf16[32,1024]{1,0:T(8,128)(2,1)})) conditional(s32[]{:T(128)} %clamp.3, (s32[16]{0:T(128)}, bf16[32,1024]{1,0:T(8,128)(2,1)}, bf16[32,1024]{1,0:T(8,128)(2,1)}, s32[8,32]{1,0:T(8,128)}, ...), branch_computations={%region_1.0_spmd, %region_2.0_spmd, %region_3.0_spmd} | conditional | bytes 8 | solution.py:736
  3.2 80.0 %branch_0_fun.1 = (bf16[2,8,240,128]{3,2,1,0:T(8,128)(2,1)}, bf16[320,2048]{1,0:T(8,128)(2,1)}, bf16[320,2048]{1,0:T(8,128)(2,1)}, bf16[32,1024]{1,0:T(8,128)(2,1)}) custom-call(s32[16]{0:T(128)} %get-tuple-element.48.match, bf16[32,1024]{1,0:T(8,128)(2,1)} %get-tuple-element.49.tokens, bf16[32,1024]{1,0:T(8,128)(2,1)} %get-tuple-element.50.cotangent, ...), custom_call_target="tpu_custom_call" | custom-call | tf_op jit(solution)/shard_map/cond/branch_0_fun/pallas_call | solution.py:663
  83.4 9.7 %shard_map.111 = (f32[1,2048,512]{2,1,0:T(8,128)}, f32[1,2048,512]{2,1,0:T(8,128)}, f32[1,2048,512]{2,1,0:T(8,128)}, bf16[32,1024]{1,0:T(8,128)(2,1)}) custom-call(bf16[2,8,240,128]{3,2,1,0:T(8,128)(2,1)} %get-tuple-element.84.landed, bf16[320,2048]{1,0:T(8,128)(2,1)} %get-tuple-element.85.rows, bf16[320,2048]{1,0:T(8,128)(2,1)} %get-tuple-element.86.grads, ...), custom_call_target="tpu_custom_call" | custom-call | tf_op jit(solution)/shard_map/pallas_call | solution.py:710

commit v3 on v2

--- a/solution.py
+++ b/solution.py
@@ -8,21 +8,14 @@
 from jax.experimental.pallas import tpu as pltpu
 from jax.sharding import PartitionSpec as P
 
-contract_rows = (((0,), (0,)), ((), ()))
 contract_cols = (((1,), (1,)), ((), ()))
 MESH = pl.DeviceIdType.MESH
 KINDS = 3
 LANES = 128
-CHUNKS = 2
 
 
 def bit_count(size):
     return size.bit_length() - 1
-
-
-def flipped(index, bit):
-    step = 2**bit
-    return index + step * (1 - 2 * ((index // step) % 2))
 
 
 def gather_orders(expert_bits, dp_bits):
@@ -37,6 +30,14 @@
         mid + far + across + last,
         far + mid + last,
     )
+
+
+def landing_order(steps, parts):
+    def turn(mask):
+        top = 2 ** (mask.bit_length() - 1)
+        return (mask - top, top)
+
+    return [(i, mask) for mask in sorted(range(1, 2 ** (steps - 1)), key=turn) for i in range(parts)]
 
 
 def reduce_orders(expert_bits, dp_bits):
@@ -74,14 +75,15 @@
         self.group_toks = self.blocks * tok_rows
         self.slots = self.groups * self.group_slots
         self.half = n_expert // 2
-        self.chunks = CHUNKS
-        self.chunk_groups = self.groups // self.chunks
-        self.col_tiles = hidden // LANES
-        self.row_split = max(1, self.half // (self.chunk_groups * self.col_tiles))
+        self.span = min(256, hidden)
+        self.spans = hidden // self.span
+        self.chunks = KINDS * self.spans
+        self.col_tiles = self.span // LANES
+        self.row_split = self.half // self.col_tiles
         unit = 16 * self.row_split
-        self.group_rows = -(-KINDS * self.group_slots // unit) * unit
-        self.piece_rows = self.group_rows // self.row_split
-        self.chunk_toks = self.total // self.chunks
+        self.padded = -(-self.slots // unit) * unit
+        self.piece_rows = self.padded // self.row_split
+        self.row_tile = min(256, self.total)
         self.steps = self.expert_bits + self.dp_bits
         self.row_parts = 2 if 2**self.steps <= 128 else 1
 
@@ -122,15 +124,18 @@
         w_up,
         w_down,
         weights,
-        places,
         p_weights,
-        p_places,
-        scaled,
+        picks,
+        p_picks,
+        gates,
+        uppers,
         backs,
         packed,
+        index,
         part,
         x_rows,
-        x_grads,
+        x_cols,
+        g_cols,
         summed,
         gsend,
         grecv,
@@ -154,23 +159,25 @@
     d = lax.axis_index("dp")
     h = e % half
     base = e - h
+    step_of = [2**b * (1 - 2 * ((e // 2**b) % 2)) for b in range(p.expert_bits)]
+    step_dp = [2**b * (1 - 2 * ((d // 2**b) % 2)) for b in range(p.dp_bits)]
     rows_half = p.tok_rows // 2
     part_rows = p.tok_rows // p.row_parts
     width = p.width
 
     def peer(axis, bit):
         if axis == "expert":
-            return (d, flipped(e, bit))
-        return (flipped(d, bit), e)
+            return (d, e + step_of[bit])
+        return (d + step_dp[bit], e)
 
     def origin(order, mask):
         at_e, at_d = e, d
         for k, (axis, bit) in enumerate(order):
             if mask >> k & 1:
                 if axis == "expert":
-                    at_e = flipped(at_e, bit)
+                    at_e = at_e + step_of[bit]
                 else:
-                    at_d = flipped(at_d, bit)
+                    at_d = at_d + step_dp[bit]
         return at_e, at_d
 
     orders = gather_orders(p.expert_bits, p.dp_bits)
@@ -212,7 +219,40 @@
     mirror = (d, (e + half) % n)
     pl.semaphore_signal(barrier, inc=1, device_id=mirror, device_id_type=MESH)
     for b in range(p.dp_bits):
-        pl.semaphore_signal(barrier, inc=1, device_id=(flipped(d, b), e), device_id_type=MESH)
+        pl.semaphore_signal(barrier, inc=1, device_id=(d + step_dp[b], e), device_id_type=MESH)
+    other = (base + half) % n
+    full = crossing == half
+
+    def cross_list(start):
+        flags, counts, count = [], [], 0
+        for i in range(half):
+            m = match[start + i]
+            flag = jnp.where((m >= start) & (m < start + half), 0, 1)
+            flags.append(flag)
+            counts.append(count)
+            count = count + flag
+        return flags, counts
+
+    if not full:
+        mine, theirs = cross_list(base), cross_list(other)
+    for k in range(half):
+        found = k
+        if not full:
+            found = 0
+            for i in range(half):
+                found = found + jnp.where((mine[0][i] == 1) & (mine[1][i] == k), i, 0)
+        m = match[base + k]
+        inside = (m >= base) & (m < base + half)
+        far = m - other
+        if not full:
+            far = 0
+            for i in range(half):
+                far = far + jnp.where(m - other == i, theirs[1][i], 0)
+        index[0, k] = found
+        index[1, k] = jnp.where(inside, m - base, 0)
+        index[2, k] = jnp.where(inside, 0, far)
+        index[3, k] = jnp.where(inside, 1, 0)
+
     pl.semaphore_wait(barrier, half + p.dp_bits)
 
     def flight(i, mask, k):
@@ -270,24 +310,19 @@
         c.start()
         loads.append(c)
 
-    def turn(mask):
-        top = 2 ** (mask.bit_length() - 1)
-        return (mask - top, top)
-
-    inner = sorted(range(1, 2 ** (steps - 1)), key=turn)
-    meta_masks = sorted(range(1, 2**p.expert_bits), key=turn)
-    for count, mask in enumerate(inner):
-        for i in range(len(sources)):
-            flights[i, mask].wait_recv()
-            send_on(i, mask)
-        if count < len(meta_masks):
-            for i in range(len(metas)):
-                meta_flights[i, meta_masks[count]].wait_recv()
-                meta_on(i, meta_masks[count])
-    for mask in meta_masks[len(inner) :]:
-        for i in range(len(metas)):
-            meta_flights[i, mask].wait_recv()
-            meta_on(i, mask)
+    meta_masks = list(range(1, 2**p.expert_bits))
+    for count, (i, mask) in enumerate(landing_order(steps, len(sources))):
+        flights[i, mask].wait_recv()
+        send_on(i, mask)
+        if count % len(sources) == len(sources) - 1 and meta_masks:
+            meta = meta_masks.pop(0)
+            for k in range(len(metas)):
+                meta_flights[k, meta].wait_recv()
+                meta_on(k, meta)
+    for meta in meta_masks:
+        for k in range(len(metas)):
+            meta_flights[k, meta].wait_recv()
+            meta_on(k, meta)
     for c in locals_:
         c.wait()
 
@@ -295,31 +330,29 @@
     tok = p.tok_rows
     at = lax.broadcasted_iota(jnp.int32, (tok, tok), 0)
     to = lax.broadcasted_iota(jnp.int32, (tok, tok), 1)
-
-    @pl.loop(0, n)
-    def _(b):
-        r = all_routes[b]
-        q = all_probs[b]
-        rows = pl.ds(pl.multiple_of(b * tok, tok), tok)
-        start = ((b % p.blocks) * p.capacity).astype(jnp.float32)
-        for who, w_ref, s_ref in ((e, weights, places), (partner, p_weights, p_places)):
-            hit = r == who
-            w = jnp.sum(jnp.where(hit, q, 0.0), axis=0, keepdims=True)
-            f = jnp.sum(jnp.where(hit, 1.0, 0.0), axis=0, keepdims=True)
-            w = jnp.broadcast_to(w, (tok, tok))
-            f = jnp.broadcast_to(f, (tok, tok))
-            w_col = jnp.sum(jnp.where(at == to, w, 0.0), axis=1, keepdims=True)
-            f_col = jnp.sum(jnp.where(at == to, f, 0.0), axis=1, keepdims=True)
-            rank = jnp.sum(jnp.where(to < at, f, 0.0), axis=1, keepdims=True)
-            s_col = jnp.where(f_col > 0.5, rank + start, -1.0)
-            w_ref[rows, :] = jnp.broadcast_to(w_col, (tok, LANES))
-            s_ref[rows, :] = jnp.broadcast_to(s_col, (tok, LANES))
-
-    def picker(s_ref, g):
-        place = s_ref[g * p.group_toks : (g + 1) * p.group_toks, :]
-        lane = lax.broadcasted_iota(jnp.int32, place.shape, 1).astype(jnp.float32)
-        hot = jnp.where(place == lane, 1.0, 0.0)
-        return jnp.transpose(hot)[: p.group_slots].astype(jnp.bfloat16)
+    before = jnp.where(at < to, 1.0, 0.0).astype(jnp.bfloat16)
+    start = (lax.broadcasted_iota(jnp.int32, (n, tok), 0) % p.blocks) * p.capacity
+    tables = []
+    for who in (e, partner):
+        hit = all_routes[...] == who
+        w = jnp.sum(jnp.where(hit, all_probs[...], 0.0), axis=1)
+        f = jnp.sum(jnp.where(hit, 1.0, 0.0), axis=1)
+        rank = jnp.dot(f.astype(jnp.bfloat16), before, preferred_element_type=jnp.float32)
+        place = jnp.where(f > 0.5, rank + start.astype(jnp.float32), -1.0)
+        tables.append((jnp.transpose(w), jnp.transpose(place)))
+    for (w, place), w_ref, pick_ref in (
+        (tables[0], weights, picks),
+        (tables[1], p_weights, p_picks),
+    ):
+        for g in range(p.groups):
+            cols = []
+            for b in range(g * p.blocks, (g + 1) * p.blocks):
+                w_ref[b * tok : (b + 1) * tok, :] = jnp.broadcast_to(w[:, b : b + 1], (tok, LANES))
+                cols.append(jnp.broadcast_to(place[:, b : b + 1], (tok, LANES)))
+            spots = jnp.concatenate(cols, axis=0)
+            lane = lax.broadcasted_iota(jnp.int32, spots.shape, 1).astype(jnp.float32)
+            hot = jnp.transpose(jnp.where(spots == lane, 1.0, 0.0))
+            pick_ref[g] = hot[: p.group_slots].astype(jnp.bfloat16)
 
     for mask in range(2 ** (steps - 1), 2**steps):
         for i in range(len(sources)):
@@ -327,54 +360,62 @@
     for c in loads:
         c.wait()
 
-    tile_rows = min(256, p.chunk_toks)
-    tile_cols = min(256, p.hidden)
-
-    def forward(c):
-        @pl.loop(0, p.chunk_toks // tile_rows)
-        def _(t):
-            first_row = pl.multiple_of(c * p.chunk_toks + t * tile_rows, tile_rows)
-            rows = pl.ds(first_row, tile_rows)
-            w = weights[rows, :][:, :1]
-            scaled[...] = (all_cot[rows, :].astype(jnp.float32) * w).astype(jnp.bfloat16)
-
-            @pl.loop(0, p.hidden // tile_cols)
-            def _(u):
-                cols = pl.ds(pl.multiple_of(u * tile_cols, tile_cols), tile_cols)
-                x = all_tok[rows, :]
-                gate = jnp.dot(x, w_gate[0, :, cols], preferred_element_type=jnp.float32)
-                upper = jnp.dot(x, w_up[0, :, cols], preferred_element_type=jnp.float32)
-                back = jnp.dot(
-                    scaled[...], w_down[0, :, cols], preferred_element_type=jnp.float32
+    tiles = p.total // p.row_tile
+    tile_bits = bit_count(tiles)
+
+    def tile_of(t):
+        return tuple((t >> (tile_bits - 1 - i)) & 1 for i in range(tile_bits))
+
+    def scale():
+        for t in range(tiles):
+            rows = slice(t * p.row_tile, (t + 1) * p.row_tile)
+            value = (all_cot[rows, :].astype(jnp.float32) * weights[rows, :][:, :1]).astype(
+                jnp.bfloat16
+            )
+            shape = part.shape[tile_bits:]
+            part[tile_of(t)] = value.reshape(shape)
+
+    def first_half(u):
+        cols = slice(u * p.span, (u + 1) * p.span)
+        for t in range(tiles):
+            rows = slice(t * p.row_tile, (t + 1) * p.row_tile)
+            x = all_tok[rows, :]
+            gate = jnp.dot(x, w_gate[0, :, cols], preferred_element_type=jnp.float32)
+            upper = jnp.dot(x, w_up[0, :, cols], preferred_element_type=jnp.float32)
+            gates[rows, :] = gate
+            uppers[rows, :] = upper
+            backs[2, rows, cols] = (gate * jax.nn.sigmoid(gate) * upper).astype(jnp.bfloat16)
+
+    def second_half(u):
+        cols = slice(u * p.span, (u + 1) * p.span)
+        for t in range(tiles):
+            rows = slice(t * p.row_tile, (t + 1) * p.row_tile)
+            grads = part[tile_of(t)].reshape(p.row_tile, p.model)
+            back = jnp.dot(grads, w_down[0, :, cols], preferred_element_type=jnp.float32)
+            gate = gates[rows, :]
+            sig = jax.nn.sigmoid(gate)
+            backs[0, rows, cols] = (
+                back * uppers[rows, :] * sig * (1.0 + gate * (1.0 - sig))
+            ).astype(jnp.bfloat16)
+            backs[1, rows, cols] = (back * gate * sig).astype(jnp.bfloat16)
+
+    def pack(c, kind, u):
+        per = p.group_slots // p.piece_rows
+        for g in range(p.groups):
+            rows = slice(g * p.group_toks, (g + 1) * p.group_toks)
+            value = backs[kind, rows, u * p.span : (u + 1) * p.span]
+            value = jnp.dot(picks[g], value, preferred_element_type=jnp.float32)
+            value = value.astype(jnp.bfloat16)
+            for t in range(p.col_tiles):
+                j = t * p.row_split + g * per
+                packed[c, j : j + per] = value[:, t * LANES : (t + 1) * LANES].reshape(
+                    per, p.piece_rows, LANES
                 )
-                sig = jax.nn.sigmoid(gate)
-                backs[0, rows, cols] = (
-                    back * upper * sig * (1.0 + gate * (1.0 - sig))
-                ).astype(jnp.bfloat16)
-                backs[1, rows, cols] = (back * gate * sig).astype(jnp.bfloat16)
-                backs[2, rows, cols] = (gate * sig * upper).astype(jnp.bfloat16)
-
-    def pack(c):
-        for gl in range(p.chunk_groups):
-            g = c * p.chunk_groups + gl
-            pick = picker(places, g)
-            rows = slice(g * p.group_toks, (g + 1) * p.group_toks)
-            kinds = [
-                jnp.dot(pick, backs[k, rows, :], preferred_element_type=jnp.float32).astype(
-                    jnp.bfloat16
-                )
-                for k in range(KINDS)
-            ]
-            spare = p.group_rows - KINDS * p.group_slots
-            if spare:
-                kinds.append(jnp.zeros((spare, p.hidden), jnp.bfloat16))
-            whole = jnp.concatenate(kinds, axis=0)
+        spare = p.row_split - p.groups * per
+        if spare:
             for t in range(p.col_tiles):
-                j = (gl * p.col_tiles + t) * p.row_split
-                piece = whole[:, t * LANES : (t + 1) * LANES]
-                packed[c, j : j + p.row_split] = piece.reshape(
-                    p.row_split, p.piece_rows, LANES
-                )
+                j = (t + 1) * p.row_split
+                packed[c, j - spare : j] = jnp.zeros((spare, p.piece_rows, LANES), jnp.bfloat16)
 
     def spread(c, o):
         to_h = (h + o) % half
@@ -414,36 +455,14 @@
     def stay_last(c):
         return pltpu.make_async_copy(ordered[c].at[h], landed.at[c, h], stay3.at[c])
 
-    def begin(c):
-        forward(c)
-        pack(c)
+    def begin(c, kind, u):
+        pack(c, kind, u)
         stay_first(c).start()
 
         @pl.loop(1, half)
         def _(o):
             spread(c, o).start()
 
-    def cross_list(start):
-        flags, before, count = [], [], 0
-        for i in range(half):
-            m = match[start + i]
-            inside = (m >= start) & (m < start + half)
-            flag = jnp.where(inside, 0, 1)
-            flags.append(flag)
-            before.append(count)
-            count = count + flag
-        return flags, before
-
-    def cross_at(listed, k):
-        flags, before = listed
-        found = 0
-        for i in range(half):
-            found = found + jnp.where((flags[i] == 1) & (before[i] == k), i, 0)
-        return found
-
-    other = (base + half) % n
-    full = crossing == half
-
     def swap_on(c):
         stay_first(c).wait()
 
@@ -454,27 +473,16 @@
         if full:
             staged[c][...] = arrived[c][...]
         else:
-            mine = cross_list(base)
             for k in range(crossing):
-                staged[c][k] = arrived[c][cross_at(mine, k)]
+                staged[c][k] = arrived[c][index[0, k]]
         swap(c).start()
 
     def collect_on(c):
         swap(c).wait_recv()
-        theirs = None if full else cross_list(other)
         for i in range(half):
-            m = match[base + i]
-            inside = (m >= base) & (m < base + half)
-            near = arrived[c][jnp.where(inside, m - base, 0)]
-            if full:
-                far_at = jnp.where(inside, 0, m - other)
-            else:
-                far_at = 0
-                for k in range(half):
-                    far_at = far_at + jnp.where(m - other == k, theirs[1][k], 0)
-                far_at = jnp.where(inside, 0, far_at)
-            far = swapped[c][far_at]
-            ordered[c][i] = jnp.where(inside, near, far)
+            near = arrived[c][index[1, i]]
+            far = swapped[c][index[2, i]]
+            ordered[c][i] = jnp.where(index[3, i] == 1, near, far)
         stay_last(c).start()
 
         @pl.loop(1, half)
@@ -535,50 +543,71 @@
                 start_step(i, s + 1)
 
     def pack_rows(src, dst, w_ref):
-        for g in range(p.groups):
-            pick = picker(p_places, g)
-            rows = slice(g * p.group_toks, (g + 1) * p.group_toks)
-            at_rows = slice(g * p.group_slots, (g + 1) * p.group_slots)
-            span = min(512, p.model)
-            for t in range(0, p.model, span):
-                x = src[rows, t : t + span]
+        span = min(512, p.model)
+
+        @pl.loop(0, p.model // span)
+        def _(t):
+            cols = pl.ds(pl.multiple_of(t * span, span), span)
+            for g in range(p.groups):
+                rows = slice(g * p.group_toks, (g + 1) * p.group_toks)
+                at_rows = slice(g * p.group_slots, (g + 1) * p.group_slots)
+                x = src[rows, cols]
                 if w_ref is not None:
                     x = (x.astype(jnp.float32) * w_ref[rows, :][:, :1]).astype(jnp.bfloat16)
-                dst[at_rows, t : t + span] = jnp.dot(
-                    pick, x, preferred_element_type=jnp.float32
+                x_rows[at_rows, :] = jnp.dot(
+                    p_picks[g], x, preferred_element_type=jnp.float32
                 ).astype(jnp.bfloat16)
-
-    for c in range(chunks):
-        begin(c)
+            dst[cols, :] = jnp.transpose(x_rows[...])
+
+    def make_part(first, last):
+        tile = min(512, p.model)
+
+        @pl.loop(first * p.model // (2 * tile), last * p.model // (2 * tile))
+        def _(t):
+            cols = pl.ds(pl.multiple_of(t * tile, tile), tile)
+            piece = lax.dot_general(
+                backs[0], w_gate[0, cols, :], contract_cols, preferred_element_type=jnp.float32
+            )
+            piece += lax.dot_general(
+                backs[1], w_up[0, cols, :], contract_cols, preferred_element_type=jnp.float32
+            )
+            shape = part.shape[:-1] + (tile,)
+            part[..., cols] = piece.astype(part.dtype).reshape(shape)
+
+    for u in range(p.spans):
+        first_half(u)
+        begin(KINDS * u, 2, u)
+        if u == 0:
+            scale()
+        second_half(u)
+        begin(KINDS * u + 1, 0, u)
+        begin(KINDS * u + 2, 1, u)
+    make_part(0, 1)
     swap_on(0)
-    tile = min(512, p.model)
-    for t in range(0, p.model, tile):
-        piece = lax.dot_general(
-            backs[0], w_gate[0, t : t + tile], contract_cols, preferred_element_type=jnp.float32
-        )
-        piece += lax.dot_general(
-            backs[1], w_up[0, t : t + tile], contract_cols, preferred_element_type=jnp.float32
-        )
-        shape = part.shape[:-1] + (tile,)
-        part[..., t : t + tile] = piece.astype(part.dtype).reshape(shape)
+    make_part(1, 2)
     for i in range(halves):
         start_step(i, 0)
-    for c in range(1, chunks):
+    for c in range(1, KINDS):
         swap_on(c)
-    pack_rows(all_tok, x_rows, None)
-    row_out = pltpu.make_async_copy(x_rows, out_rows, osem.at[0])
+    next_step(0)
+    for c in range(KINDS, chunks):
+        swap_on(c)
+    pack_rows(all_tok, x_cols, None)
+    row_out = pltpu.make_async_copy(x_cols, out_rows, osem.at[0])
     row_out.start()
-    next_step(0)
-    pack_rows(all_cot, x_grads, p_weights)
-    grad_out = pltpu.make_async_copy(x_grads, out_grads, osem.at[1])
-    grad_out.start()
-    next_step(1)
-    collect_on(0)
-    for s in range(2, steps - 1):
-        next_step(s)
-    for c in range(1, chunks):
-        collect_on(c)
-    next_step(steps - 1)
+    pace = 42 * crossing / (half * chunks)
+    events = [(10 + pace * (c + 1), 0, c) for c in range(chunks)]
+    events += [(13.5 + 5.5 * s, 1, s) for s in range(1, steps)]
+    events.append((10 + 1.1 * pace, 2, 0))
+    for _, kind, which in sorted(events):
+        if kind == 0:
+            collect_on(which)
+        elif kind == 1:
+            next_step(which)
+        else:
+            pack_rows(all_cot, g_cols, p_weights)
+            grad_out = pltpu.make_async_copy(g_cols, out_grads, osem.at[1])
+            grad_out.start()
     for i in range(halves):
         summed[pl.ds(i * rows_half, rows_half), :] = sums[i][steps - 1][...]
     result_out = pltpu.make_async_copy(summed, result, osem.at[2])
@@ -631,14 +660,17 @@
             pltpu.VMEM(weight, dtype),
             pltpu.VMEM((p.total, LANES), jnp.float32),
             pltpu.VMEM((p.total, LANES), jnp.float32),
-            pltpu.VMEM((p.total, LANES), jnp.float32),
-            pltpu.VMEM((p.total, LANES), jnp.float32),
-            pltpu.VMEM((min(256, p.chunk_toks), p.model), dtype),
+            pltpu.VMEM((p.groups, p.group_slots, p.group_toks), dtype),
+            pltpu.VMEM((p.groups, p.group_slots, p.group_toks), dtype),
+            pltpu.VMEM((p.total, p.span), jnp.float32),
+            pltpu.VMEM((p.total, p.span), jnp.float32),
             pltpu.VMEM((KINDS, p.total, p.hidden), dtype),
             pltpu.VMEM((chunks, half) + piece, dtype),
+            pltpu.SMEM((4, half), jnp.int32),
             pltpu.VMEM((2,) * p.expert_bits + (p.tok_rows, p.model), dtype),
-            pltpu.VMEM((p.slots, p.model), dtype),
-            pltpu.VMEM((p.slots, p.model), dtype),
+            pltpu.VMEM((p.slots, min(512, p.model)), dtype),
+            pltpu.VMEM((p.model, p.slots), dtype),
+            pltpu.VMEM((p.model, p.slots), dtype),
             pltpu.VMEM((p.tok_rows, p.width), dtype),
             dma((2 * p.row_parts, 2**steps)),
             dma((2 * p.row_parts, 2**steps)),
@@ -664,8 +696,8 @@
         functools.partial(comm_kernel, p, crossing),
         out_shape=(
             jax.ShapeDtypeStruct((chunks, half) + piece, dtype),
-            jax.ShapeDtypeStruct((p.slots, p.model), dtype),
-            jax.ShapeDtypeStruct((p.slots, p.model), dtype),
+            jax.ShapeDtypeStruct((p.model, p.slots), dtype),
+            jax.ShapeDtypeStruct((p.model, p.slots), dtype),
             jax.ShapeDtypeStruct((p.tok_rows, p.width), dtype),
         ),
         in_specs=[pl.BlockSpec(memory_space=pltpu.SMEM)] + [anywhere] * 7,
@@ -677,36 +709,68 @@
     )(*operands)
 
 
-def final_kernel(p, landed, rows, grads, summed, g_gate, g_up, g_down, out, acts):
-    @pl.when(pl.program_id(0) == 0)
-    def _():
-        out[...] = summed[...]
-        for c in range(p.chunks):
-            for gl in range(p.chunk_groups):
-                at = (c * p.chunk_groups + gl) * p.group_slots
-                for t in range(p.col_tiles):
-                    j = (gl * p.col_tiles + t) * p.row_split
-                    piece = landed[c, j : j + p.row_split].reshape(p.group_rows, LANES)
-                    for k in range(KINDS):
-                        acts[k, at : at + p.group_slots, t * LANES : (t + 1) * LANES] = piece[
-                            k * p.group_slots : (k + 1) * p.group_slots
-                        ]
-
-    x = rows[...]
-    g_gate[0] = lax.dot_general(x, acts[0], contract_rows, preferred_element_type=jnp.float32)
-    g_up[0] = lax.dot_general(x, acts[1], contract_rows, preferred_element_type=jnp.float32)
-    g_down[0] = lax.dot_general(
-        grads[...], acts[2], contract_rows, preferred_element_type=jnp.float32
-    )
+def final_kernel(
+    p, landed, rows, grads, summed, g_gate, g_up, g_down, out, items, x, g, small, acts, sums,
+    item_sem, x_sem, g_sem, small_sem, out_sem,
+):
+    tile = min(256, p.model)
+    count = p.model // tile
+    item_in = pltpu.make_async_copy(landed, items, item_sem)
+    item_in.start()
+
+    def load(i):
+        at = pl.ds(pl.multiple_of(i * tile, tile), tile)
+        return (
+            pltpu.make_async_copy(rows.at[at], x.at[at], x_sem.at[i]),
+            pltpu.make_async_copy(grads.at[at], g.at[at], g_sem.at[i]),
+        )
+
+    def store(i):
+        at = pl.ds(pl.multiple_of(i * tile, tile), tile)
+        return [
+            pltpu.make_async_copy(sums.at[k, at], dst.at[0, at], out_sem.at[k, i])
+            for k, dst in enumerate((g_gate, g_up, g_down))
+        ]
+
+    for i in range(count):
+        for c in load(i):
+            c.start()
+    small_in = pltpu.make_async_copy(summed, small, small_sem.at[0])
+    small_in.start()
+    item_in.wait()
+    for u in range(p.spans):
+        for i, kind in enumerate((2, 0, 1)):
+            for t in range(p.col_tiles):
+                at = u * p.span + t * LANES
+                piece = items[KINDS * u + i, t * p.row_split : (t + 1) * p.row_split]
+                acts[kind, :, at : at + LANES] = piece.reshape(p.padded, LANES)[: p.slots]
+    small_in.wait()
+    small_out = pltpu.make_async_copy(small, out, small_sem.at[1])
+    small_out.start()
+
+    @pl.loop(0, count)
+    def _(i):
+        at = pl.ds(pl.multiple_of(i * tile, tile), tile)
+        for c in load(i):
+            c.wait()
+        for k, src in enumerate((x, x, g)):
+            sums[k, at, :] = jnp.dot(src[at, :], acts[k], preferred_element_type=jnp.float32)
+        for c in store(i):
+            c.start()
+
+    small_out.wait()
+
+    @pl.loop(0, count)
+    def _(i):
+        for c in store(i):
+            c.wait()
 
 
 def finish(p, landed, rows, grads, summed):
     tile = min(256, p.model)
-    wide = pl.BlockSpec((p.slots, tile), lambda i: (0, i))
-    grad = pl.BlockSpec((1, tile, p.hidden), lambda i: (0, i, 0))
     grad_shape = jax.ShapeDtypeStruct((1, p.model, p.hidden), jnp.float32)
-    whole = pl.BlockSpec(landed.shape, lambda i: (0, 0, 0, 0))
-    small = pl.BlockSpec(summed.shape, lambda i: (0, 0))
+    anywhere = pl.BlockSpec(memory_space=pl.ANY)
+    dma = pltpu.SemaphoreType.DMA
     return pl.pallas_call(
         functools.partial(final_kernel, p),
         out_shape=(
@@ -715,10 +779,21 @@
             grad_shape,
             jax.ShapeDtypeStruct(summed.shape, summed.dtype),
         ),
-        grid=(p.model // tile,),
-        in_specs=[whole, wide, wide, small],
-        out_specs=[grad, grad, grad, small],
-        scratch_shapes=[pltpu.VMEM((KINDS, p.slots, p.hidden), landed.dtype)],
+        in_specs=[anywhere] * 4,
+        out_specs=[anywhere] * 4,
+        scratch_shapes=[
+            pltpu.VMEM(landed.shape, landed.dtype),
+            pltpu.VMEM(rows.shape, rows.dtype),
+            pltpu.VMEM(grads.shape, grads.dtype),
+            pltpu.VMEM(summed.shape, summed.dtype),
+            pltpu.VMEM((KINDS, p.slots, p.hidden), landed.dtype),
+            pltpu.VMEM((KINDS, p.model, p.hidden), jnp.float32),
+            dma,
+            dma((p.model // tile,)),
+            dma((p.model // tile,)),
+            dma((2,)),
+            dma((KINDS, p.model // tile)),
+        ],
     )(landed, rows, grads, summed)
 
 

time: 94.7 us -> 85.1 us (0.90); the launches traced: 93.2 us -> 85 us
  Pallas kernels: 89.7 us -> 81.3 us
    pallas_call x1, Pallas kernels: 80 us -> 72.9 us  [communicate(): pl.pallas_call(functools.partial(comm_kernel, p, crossing), out_shape=(ja...]
    pallas_call x1, Pallas kernels: 9.73 us -> 8.36 us  [finish(): pl.pallas_call(functools.partial(final_kernel, p), out_shape=(grad_shape,...]
where the time goes in v3:
time: 85.1 us; the launch traced here: 85 us
  Pallas kernels  81.3 us (96%)
  between operations  2.12 us (2%)
  other arithmetic  1.29 us (2%)
    pallas_call x1, Pallas kernels, communicate(): pl.pallas_call(functools.partial(comm_kernel, p, crossing), out_shape=(ja...  72.9 us
    pallas_call x1, Pallas kernels, finish(): pl.pallas_call(functools.partial(final_kernel, p), out_shape=(grad_shape,...  8.36 us

profile of v3, /device:TPU:0, one launch (start us, length us, event | category | flops | bytes accessed | tf_op | source)
XLA Modules:
  0.0 85.0 jit_solution(8282452374439598578)
XLA Ops:
  0.6 1.3 %fusion = s32[]{:T(128)} fusion(s32[16]{0:T(128)} %param.15), kind=kLoop, calls=%fused_computation.1 | loop fusion | flops 23 | bytes 36 | tf_op jit(solution)/shard_map/reduce_sum | solution.py:805
  3.2 73.2 %conditional.1 = ((bf16[6,8,80,128]{3,2,1,0:T(8,128)(2,1)}, bf16[2048,320]{1,0:T(8,128)(2,1)}, bf16[2048,320]{1,0:T(8,128)(2,1)}, bf16[32,1024]{1,0:T(8,128)(2,1)})) conditional(s32[]{:T(128)} %clamp.3, (s32[16]{0:T(128)}, bf16[32,1024]{1,0:T(8,128)(2,1)}, bf16[32,1024]{1,0:T(8,128)(2,1)}, s32[8,32]{1,0:T(8,128)}, ...), branch_computations={%region_1.0_spmd, %region_2.0_spmd, %region_3.0_spmd} | conditional | bytes 8 | solution.py:811
  3.2 72.9 %branch_0_fun.1 = (bf16[6,8,80,128]{3,2,1,0:T(8,128)(2,1)}, bf16[2048,320]{1,0:T(8,128)(2,1)}, bf16[2048,320]{1,0:T(8,128)(2,1)}, bf16[32,1024]{1,0:T(8,128)(2,1)}) custom-call(s32[16]{0:T(128)} %get-tuple-element.48.match, bf16[32,1024]{1,0:T(8,128)(2,1)} %get-tuple-element.49.tokens, bf16[32,1024]{1,0:T(8,128)(2,1)} %get-tuple-element.50.cotangent, ...), custom_call_target="tpu_custom_call" | custom-call | tf_op jit(solution)/shard_map/cond/branch_0_fun/pallas_call | solution.py:695
  76.4 8.4 %shard_map.111 = (f32[1,2048,512]{2,1,0:T(8,128)}, f32[1,2048,512]{2,1,0:T(8,128)}, f32[1,2048,512]{2,1,0:T(8,128)}, bf16[32,1024]{1,0:T(8,128)(2,1)}) custom-call(bf16[6,8,80,128]{3,2,1,0:T(8,128)(2,1)} %get-tuple-element.84.landed, bf16[2048,320]{1,0:T(8,128)(2,1)} %get-tuple-element.85.rows, bf16[2048,320]{1,0:T(8,128)(2,1)} %get-tuple-element.86.grads, ...), custom_call_target="tpu_custom_call" | custom-call | tf_op jit(solution)/shard_map/pallas_call | solution.py:774

commit v4 on v3

--- a/solution.py
+++ b/solution.py
@@ -300,10 +300,13 @@
             c.start()
             meta_flights[i, mask + 2**k] = c
 
-    for i in range(len(sources)):
-        send_on(i, 0)
     for i in range(len(metas)):
         meta_on(i, 0)
+    for k in range(steps):
+        for i in range(len(sources)):
+            c = flight(i, 0, k)
+            c.start()
+            flights[i, 2**k] = c
     loads = []
     for i, (src, dst) in enumerate(((h_gate, w_gate), (h_up, w_up), (h_down, w_down))):
         c = pltpu.make_async_copy(src, dst, wsem.at[i])
@@ -597,7 +600,7 @@
     row_out.start()
     pace = 42 * crossing / (half * chunks)
     events = [(10 + pace * (c + 1), 0, c) for c in range(chunks)]
-    events += [(13.5 + 5.5 * s, 1, s) for s in range(1, steps)]
+    events += [(12 + 6.5 * s, 1, s) for s in range(1, steps)]
     events.append((10 + 1.1 * pace, 2, 0))
     for _, kind, which in sorted(events):
         if kind == 0:
@@ -713,7 +716,7 @@
     p, landed, rows, grads, summed, g_gate, g_up, g_down, out, items, x, g, small, acts, sums,
     item_sem, x_sem, g_sem, small_sem, out_sem,
 ):
-    tile = min(256, p.model)
+    tile = min(512, p.model)
     count = p.model // tile
     item_in = pltpu.make_async_copy(landed, items, item_sem)
     item_in.start()
@@ -753,10 +756,10 @@
         at = pl.ds(pl.multiple_of(i * tile, tile), tile)
         for c in load(i):
             c.wait()
+        outs = store(i)
         for k, src in enumerate((x, x, g)):
             sums[k, at, :] = jnp.dot(src[at, :], acts[k], preferred_element_type=jnp.float32)
-        for c in store(i):
-            c.start()
+            outs[k].start()
 
     small_out.wait()
 
@@ -767,7 +770,7 @@
 
 
 def finish(p, landed, rows, grads, summed):
-    tile = min(256, p.model)
+    tile = min(512, p.model)
     grad_shape = jax.ShapeDtypeStruct((1, p.model, p.hidden), jnp.float32)
     anywhere = pl.BlockSpec(memory_space=pl.ANY)
     dma = pltpu.SemaphoreType.DMA
@@ -802,8 +805,10 @@
     p = Plan(n_expert, n_dp, tok_rows, tokens.shape[1], top_count, w_gate.shape[2])
     operands = (matching, tokens, cotangent, routes.T, probs.T, w_gate, w_up, w_down)
     sizes = (p.half // 2, 3 * p.half // 4, p.half)
-    pairs = jnp.sum((matching[: p.half] >= p.half).astype(jnp.int32))
-    which = sum((pairs > size).astype(jnp.int32) for size in sizes[:-1])
+    low = jnp.arange(n_expert) < p.half
+    crossed = jnp.sum((low != (matching < p.half)).astype(jnp.int32))
+    over = jnp.maximum(crossed - (p.half // 2 + 1), 0)
+    which = lax.shift_right_logical(over, bit_count(p.half // 2))
     calls = [
         functools.partial(lambda size, i, *a: communicate(p, size, i, a), size, i)
         for i, size in enumerate(sizes)

time: 85.1 us -> 83.1 us (0.976)
  Pallas kernels: 81.3 us -> 79.9 us
    pallas_call x1, Pallas kernels: 8.36 us -> 7.28 us  [finish(): pl.pallas_call(functools.partial(final_kernel, p), out_shape=(grad_shape,...]
where the time goes in v4:
time: 83.1 us; the launch traced here: 82.9 us
  Pallas kernels  79.9 us (96%)
  between operations  1.47 us (2%)
  other arithmetic  1.3 us (2%)
    pallas_call x1, Pallas kernels, communicate(): pl.pallas_call(functools.partial(comm_kernel, p, crossing), out_shape=(ja...  72.6 us
    pallas_call x1, Pallas kernels, finish(): pl.pallas_call(functools.partial(final_kernel, p), out_shape=(grad_shape,...  7.28 us

profile of v4, /device:TPU:0, one launch (start us, length us, event | category | flops | bytes accessed | tf_op | source)
XLA Modules:
  0.0 82.9 jit_solution(2791916087277378568)
XLA Ops:
  0.6 1.3 %fusion = s32[]{:T(128)} fusion(s32[16]{0:T(128)} %param.15), kind=kLoop, calls=%fused_computation.1 | loop fusion | flops 79 | bytes 68 | tf_op jit(solution)/shard_map/reduce_sum | solution.py:809
  2.6 72.8 %conditional.1 = ((bf16[6,8,80,128]{3,2,1,0:T(8,128)(2,1)}, bf16[2048,320]{1,0:T(8,128)(2,1)}, bf16[2048,320]{1,0:T(8,128)(2,1)}, bf16[32,1024]{1,0:T(8,128)(2,1)})) conditional(s32[]{:T(128)} %clamp.3, (s32[16]{0:T(128)}, bf16[32,1024]{1,0:T(8,128)(2,1)}, bf16[32,1024]{1,0:T(8,128)(2,1)}, s32[8,32]{1,0:T(8,128)}, ...), branch_computations={%region_1.0_spmd, %region_2.0_spmd, %region_3.0_spmd} | conditional | bytes 8 | solution.py:816
  2.6 72.6 %branch_0_fun.1 = (bf16[6,8,80,128]{3,2,1,0:T(8,128)(2,1)}, bf16[2048,320]{1,0:T(8,128)(2,1)}, bf16[2048,320]{1,0:T(8,128)(2,1)}, bf16[32,1024]{1,0:T(8,128)(2,1)}) custom-call(s32[16]{0:T(128)} %get-tuple-element.48.match, bf16[32,1024]{1,0:T(8,128)(2,1)} %get-tuple-element.49.tokens, bf16[32,1024]{1,0:T(8,128)(2,1)} %get-tuple-element.50.cotangent, ...), custom_call_target="tpu_custom_call" | custom-call | tf_op jit(solution)/shard_map/cond/branch_0_fun/pallas_call | solution.py:698
  75.4 7.3 %shard_map.111 = (f32[1,2048,512]{2,1,0:T(8,128)}, f32[1,2048,512]{2,1,0:T(8,128)}, f32[1,2048,512]{2,1,0:T(8,128)}, bf16[32,1024]{1,0:T(8,128)(2,1)}) custom-call(bf16[6,8,80,128]{3,2,1,0:T(8,128)(2,1)} %get-tuple-element.84.landed, bf16[2048,320]{1,0:T(8,128)(2,1)} %get-tuple-element.85.rows, bf16[2048,320]{1,0:T(8,128)(2,1)} %get-tuple-element.86.grads, ...), custom_call_target="tpu_custom_call" | custom-call | tf_op jit(solution)/shard_map/pallas_call | solution.py:777
